TPU v7x, 128 devices: a whole 4x4x4 slice. The times are simulated.
128 devices in a mesh: leaf: 128 (over x, y, z, core).
Axes of the slice: x: 4, y: 4, z: 4, core: 2. Of those that a mesh axis runs over, the one named last changes fastest.
Arguments:
- points: bfloat16 [131072, 768], P('leaf'), may hold values from -4 to 4
- weights: bfloat16 [131072, 64], P('leaf'), may hold values from -0.0390625 to 0.0390625
- tree_slot: int32 [131072], P('leaf'), may hold values from 0 to 131071, as said below
- leaf_interp: bfloat16 [128, 256, 1024], P('leaf'), may hold values from -0.1875 to 0.1875
- skel_leaf: int32 [128, 256], P('leaf'), may hold values from 0 to 1023, as said below
- merge_interp: bfloat16 [128, 240, 512], P('leaf'), may hold values from -0.25 to 0.25
- merge_index: int32 [128, 240], P('leaf'), may hold values from 0 to 511, as said below
- near_mask: int32 [128, 8], P('leaf'), may hold values from 0 to 1, as said below
- far_mask: int32 [128, 4, 4], P('leaf'), may hold values from 0 to 1, as said below
Outputs:
- sums: float32 [131072, 64], P('leaf')
Inputs may be any that keep to these rules, and one draw needn't show every extreme that they name: `tree_slot`: A permutation of the tree positions; each aligned block of 1024 input points sends exactly 8 points into the block of every leaf. `skel_leaf`: each row lists 256 distinct positions. `merge_index`: for every node of every level, the 256 entries of I_k are distinct. Symmetric: near_mask[l, 4 + s - 1] equals near_mask[l + s, 4 - s] for 1 <= s <= 4; entries that name a leaf outside the tree are 0. `far_mask`: entries that name a node outside its level are 0.
All inputs are finite; a program needn't handle non-finite values.
Results may differ from a plain program's by a relative error of at most 0.0042.
Values may be sent and summed in bfloat16 or wider, within the bound.
A program may use at most 128 MiB of HBM per device.

v0:
```python
import math

import jax
import jax.numpy as jnp
from jax import lax
from jax.sharding import PartitionSpec as P

LEVELS = 4
NWIN = 4
FWIN = 2


def from_partner(value, axis, stride):
    mask = 2**stride
    pairs = [(source, source ^ mask) for source in range(lax.axis_size(axis))]
    return lax.ppermute(value, axis, pairs)


def from_behind(value, axis, by):
    devices = lax.axis_size(axis)
    pairs = [(i, i + by) for i in range(devices) if 0 <= i + by < devices]
    return lax.ppermute(value, axis, pairs)


def row_offset(block, scale_inv):
    squares = jnp.sum(jnp.square(block.astype(jnp.float32)), axis=1)
    return (squares - block.shape[1]) * (0.5 * scale_inv)


def kernel_block(targets, target_shift, sources, source_shift, scale_inv):
    products = jnp.dot(targets, sources.T, preferred_element_type=jnp.float32)
    exponent = products * scale_inv - target_shift[:, None] - source_shift[None, :]
    return jnp.exp(exponent).astype(jnp.bfloat16)


def join_halves(is_high, mine, other):
    return jnp.where(
        is_high, jnp.concatenate([other, mine], axis=0), jnp.concatenate([mine, other], axis=0)
    )


def local(
    points,
    weights,
    tree_slot,
    leaf_interp,
    skel_leaf,
    merge_interp,
    merge_index,
    near_mask,
    far_mask,
):
    leaf_count = lax.axis_size("leaf")
    position = lax.axis_index("leaf")
    local_rows, feature_width = points.shape
    column_count = weights.shape[1]
    scale_inv = 1.0 / (1.75 * math.sqrt(feature_width))
    per_peer = local_rows // leaf_count
    by_dest = jnp.argsort(tree_slot)
    send_points = points[by_dest].reshape(leaf_count, per_peer, feature_width)
    send_weights = weights[by_dest].reshape(leaf_count, per_peer, column_count)
    send_slots = tree_slot[by_dest].reshape(leaf_count, per_peer)
    got_points, got_weights, got_slots = (
        lax.all_to_all(send_points, "leaf", split_axis=0, concat_axis=0, tiled=True),
        lax.all_to_all(send_weights, "leaf", split_axis=0, concat_axis=0, tiled=True),
        lax.all_to_all(send_slots, "leaf", split_axis=0, concat_axis=0, tiled=True),
    )
    tree_place = (got_slots.reshape(-1) % local_rows).astype(jnp.int32)
    arrange = jnp.argsort(tree_place)
    tree_pts = got_points.reshape(local_rows, feature_width)[arrange]
    tree_wts = got_weights.reshape(local_rows, column_count)[arrange]
    own_shift = row_offset(tree_pts, scale_inv)

    def evaluate(operands):
        kernel = kernel_block(
            tree_pts, own_shift, operands[0], row_offset(operands[0], scale_inv), scale_inv
        )
        return jnp.dot(kernel, operands[1], preferred_element_type=jnp.float32)

    def nothing(operands):
        return jnp.zeros((local_rows, column_count), jnp.float32)

    outputs = evaluate((tree_pts, tree_wts))
    rank_rows = skel_leaf.shape[1]
    node_pts = tree_pts[skel_leaf[0]]
    node_wts = jnp.dot(leaf_interp[0], tree_wts, preferred_element_type=jnp.float32).astype(
        jnp.bfloat16
    )
    far_steps = list(range(-FWIN, 0)) + list(range(1, FWIN + 1))
    offset = 0
    for tree_level in range(1, LEVELS + 1):
        sib_pts, sib_wts = from_partner((node_pts, node_wts), "leaf", tree_level - 1)
        is_upper = jnp.bitwise_and(jnp.right_shift(position, tree_level - 1), 1) == 1
        both_pts = join_halves(is_upper, node_pts, sib_pts)
        both_wts = join_halves(is_upper, node_wts, sib_wts)
        piece_rows = rank_rows >> tree_level
        piece_interp = merge_interp[0, offset : offset + piece_rows]
        piece_index = merge_index[0, offset : offset + piece_rows]
        part_wts = jnp.dot(piece_interp, both_wts, preferred_element_type=jnp.float32).astype(
            jnp.bfloat16
        )
        part_pts = both_pts[piece_index]
        for bit_place in range(tree_level):
            other_pts, other_wts = from_partner((part_pts, part_wts), "leaf", bit_place)
            is_high = jnp.bitwise_and(jnp.right_shift(position, bit_place), 1) == 1
            part_pts = join_halves(is_high, part_pts, other_pts)
            part_wts = join_halves(is_high, part_wts, other_wts)
        node_pts = part_pts
        node_wts = part_wts
        offset += piece_rows
        for column, node_step in enumerate(far_steps):
            far_pts, far_wts = from_behind(
                (node_pts, node_wts), "leaf", -node_step * (1 << tree_level)
            )
            outputs = outputs + lax.cond(
                far_mask[0, tree_level - 1, column] > 0, evaluate, nothing, (far_pts, far_wts)
            )
    near_steps = list(range(-NWIN, 0)) + list(range(1, NWIN + 1))
    for column, leaf_step in enumerate(near_steps):
        near_pts, near_wts = from_behind((tree_pts, tree_wts), "leaf", -leaf_step)
        outputs = outputs + lax.cond(
            near_mask[0, column] > 0, evaluate, nothing, (near_pts, near_wts)
        )
    send_back = outputs[tree_place].reshape(leaf_count, per_peer, column_count)
    home_rows = lax.all_to_all(send_back, "leaf", split_axis=0, concat_axis=0, tiled=True)
    undo_order = jnp.argsort(by_dest)
    return home_rows.reshape(local_rows, column_count)[undo_order]


def solution(mesh):
    placed = (
        P("leaf", None),
        P("leaf", None),
        P("leaf"),
        P("leaf", None, None),
        P("leaf", None),
        P("leaf", None, None),
        P("leaf", None),
        P("leaf", None),
        P("leaf", None, None),
    )
    return jax.shard_map(
        local, mesh=mesh, in_specs=placed, out_specs=P("leaf", None), check_vma=False
    )
```

profile of v0, /device:TPU:1, one launch (start us, length us, event | category | flops | bytes accessed | tf_op | source)
XLA Modules:
  0.0 708.1 jit_solution(1106881102755127336)
XLA Ops:
  0.0 5.2 sort.45
  5.2 4.5 gather_fusion.1
  10.5 11.5 %all-to-all-start.1 = ((s32[128,1,8]{2,1,0:T(1,128)}), s32[128,1,8]{2,1,0:T(1,128)S(1)}, u32[]{:S(2)}, u32[]{:S(2)}) async-start(s32[128,1,8]{2,1,0:T(1,128)} %bitcast.2), calls=%async_computation.1 | async-start | bytes 131072 | tf_op jit(solution)/shard_map/all_to_all | solution.py:66
  26.2 5.1 all-to-all-done.1
  31.3 4.8 all-to-all-start.2
  36.1 5.2 gather_fusion
  45.8 6.8 all-to-all-start
  52.6 4.4 sort.46
  57.2 4.3 gather_fusion.4
  68.7 5.1 collective-permute-done.16
  77.4 5.2 gather_fusion.2
  102.4 4.6 collective-permute-start.7
  139.9 10.0 %collective-permute-done.75 = bf16[1024,64]{1,0:T(8,128)(2,1)S(1)} collective-permute-done((bf16[1024,64]{1,0:T(8,128)(2,1)}, bf16[1024,64]{1,0:T(8,128)(2,1)S(1)}, u32[]{:S(2)}, u32[]{:S(2)}) %collective-permute-start.75) | collective-permute-done | bytes 131104 | tf_op jit(solution)/shard_map/ppermute | solution.py:22
  149.9 4.6 collective-permute-start.67
  154.5 8.7 %collective-permute-start.65 = (bf16[1024,64]{1,0:T(8,128)(2,1)}, bf16[1024,64]{1,0:T(8,128)(2,1)}, u32[]{:S(2)}, u32[]{:S(2)}) collective-permute-start(bf16[1024,64]{1,0:T(8,128)(2,1)} %gather_fusion.4), channel_id=1, source_target_pairs={{0,2},{1,3},{2,4},{3,5},{4,6},{5,7},{6,8},{7,9},{8,10},{9,11},{10,... | collective-permute-start | bytes 393224 | tf_op jit(solution)/shard_map/ppermute | solution.py:22
  183.1 5.5 collective-permute-start.21
  194.3 8.0 %collective-permute-start.19 = (bf16[256,64]{0,1:T(8,128)(2,1)}, bf16[256,64]{0,1:T(8,128)(2,1)S(1)}, u32[]{:S(2)}, u32[]{:S(2)}) collective-permute-start(bf16[256,64]{0,1:T(8,128)(2,1)} %copy-done.14), channel_id=1, source_target_pairs={{0,8},{1,9},{2,10},{3,11},{4,12},{5,13},{6,14},{7,15},{8,16},{9,17... | collective-permute-start | bytes 98312 | tf_op jit(solution)/shard_map/ppermute | solution.py:22
  205.1 4.7 collective-permute-done.41
  209.8 61.6 %collective-permute-start.37 = (bf16[256,64]{1,0:T(8,128)(2,1)}, bf16[256,64]{1,0:T(8,128)(2,1)S(1)}, u32[]{:S(2)}, u32[]{:S(2)}) collective-permute-start(bf16[256,64]{1,0:T(8,128)(2,1)} %copy-done.13), channel_id=1, source_target_pairs={{0,8},{1,9},{2,10},{3,11},{4,12},{5,13},{6,14},{7,15},{8,16},{9,17... | collective-permute-start | bytes 98312 | tf_op jit(solution)/shard_map/ppermute | solution.py:22
  273.0 4.7 collective-permute-start.35
  281.1 9.7 %collective-permute-done.59 = bf16[256,64]{1,0:T(8,128)(2,1)S(1)} collective-permute-done((bf16[256,64]{1,0:T(8,128)(2,1)}, bf16[256,64]{1,0:T(8,128)(2,1)S(1)}, u32[]{:S(2)}, u32[]{:S(2)}) %collective-permute-start.59) | collective-permute-done | bytes 32800 | tf_op jit(solution)/shard_map/ppermute | solution.py:22
  292.1 5.5 collective-permute-done.57
  300.9 5.4 collective-permute-done.8
  308.8 33.9 %collective-permute-done.42 = bf16[256,768]{1,0:T(8,128)(2,1)S(1)} collective-permute-done((bf16[256,768]{1,0:T(8,128)(2,1)S(1)}, bf16[256,768]{1,0:T(8,128)(2,1)S(1)}, u32[]{:S(2)}, u32[]{:S(2)}) %collective-permute-start.42) | collective-permute-done | bytes 393248 | tf_op jit(solution)/shard_map/ppermute | solution.py:16
  348.4 6.9 collective-permute-start.43
  362.9 5.1 collective-permute-start.64
  368.1 16.8 %collective-permute-start.62 = (bf16[1024,768]{1,0:T(8,128)(2,1)S(1)}, bf16[1024,768]{1,0:T(8,128)(2,1)}, u32[]{:S(2)}, u32[]{:S(2)}) collective-permute-start(bf16[1024,768]{1,0:T(8,128)(2,1)S(1)} %copy-done.2), channel_id=1, source_target_pairs={{0,3},{1,4},{2,5},{3,6},{4,7},{5,8},{6,9},{7,10},{8,11},{9,12},{10... | collective-permute-start | bytes 4718600 | tf_op jit(solution)/shard_map/ppermute | solution.py:22
  385.0 71.7 %collective-permute-done.45 = bf16[64,768]{1,0:T(8,128)(2,1)S(1)} collective-permute-done((bf16[64,768]{1,0:T(8,128)(2,1)S(1)}, bf16[64,768]{1,0:T(8,128)(2,1)S(1)}, u32[]{:S(2)}, u32[]{:S(2)}) %collective-permute-start.45) | collective-permute-done | bytes 98336 | tf_op jit(solution)/shard_map/ppermute | solution.py:16
  456.7 6.9 collective-permute-start.60
  485.7 5.5 collective-permute-start.20
  500.0 17.1 %collective-permute-start.36 = (bf16[256,768]{1,0:T(8,128)(2,1)}, bf16[256,768]{1,0:T(8,128)(2,1)}, u32[]{:S(2)}, u32[]{:S(2)}) collective-permute-start(bf16[256,768]{1,0:T(8,128)(2,1)} %copy-done.4), channel_id=1, source_target_pairs={{0,8},{1,9},{2,10},{3,11},{4,12},{5,13},{6,14},{7,15},{8,16},{9,17... | collective-permute-start | bytes 1179656 | tf_op jit(solution)/shard_map/ppermute | solution.py:22
  521.6 5.8 collective-permute-start.55
  527.4 4.9 collective-permute-start.53
  533.6 6.2 collective-permute-start.54
  539.8 6.1 collective-permute-start.47
  555.4 6.5 conditional.47
  557.2 4.7 fusion.158
  561.9 6.5 conditional.46
  563.7 4.7 fusion.156
  568.4 6.5 conditional.45
  570.2 4.7 fusion.154
  574.9 6.9 conditional.44
  577.1 4.7 fusion.152
  581.8 6.5 conditional.43
  583.6 4.7 fusion.150
  619.2 72.3 %all-to-all-start.3 = ((f32[128,1,512]{2,1,0:T(1,128)}), f32[128,1,512]{2,1,0:T(1,128)S(1)}, u32[]{:S(2)}, u32[]{:S(2)}) async-start(f32[128,1,512]{2,1,0:T(1,128)} %reshape.602), calls=%async_computation.3 | async-start | bytes 524288 | tf_op jit(solution)/shard_map/all_to_all | solution.py:125
  691.5 4.4 sort.47
  695.9 6.4 all-to-all-done.3
  (343 shorter events, 230.7 us)
Async XLA Ops:
  10.5 20.9 %all-to-all-start.1 = ((s32[128,1,8]{2,1,0:T(1,128)}), s32[128,1,8]{2,1,0:T(1,128)S(1)}, u32[]{:S(2)}, u32[]{:S(2)}) async-start(s32[128,1,8]{2,1,0:T(1,128)} %bitcast.2), calls=%async_computation.1 | async-start | bytes 131072 | tf_op jit(solution)/shard_map/all_to_all | solution.py:66
  45.8 31.6 %all-to-all-start = ((bf16[128,8,768]{2,1,0:T(8,128)(2,1)}), bf16[128,8,768]{2,1,0:T(8,128)(2,1)S(1)}, u32[]{:S(2)}, u32[]{:S(2)}) async-start(bf16[128,8,768]{2,1,0:T(8,128)(2,1)} %bitcast.156), calls=%async_computation | async-start | bytes 3145728 | tf_op jit(solution)/shard_map/all_to_all | solution.py:64
  99.8 32.2 %collective-permute-start.11 = (bf16[256,64]{0,1:T(8,128)(2,1)}, bf16[256,64]{0,1:T(8,128)(2,1)}, u32[]{:S(2)}, u32[]{:S(2)}) collective-permute-start(bf16[256,64]{0,1:T(8,128)(2,1)} %maximum_select_fusion.24), channel_id=1, source_target_pairs={{4,0},{5,1},{6,2},{7,3},{8,4},{9,5},{10,6},{11,7},{12,8},{13,9},{1... | collective-permute-start | bytes 98312 | tf_op jit(solution)/shard_map/ppermute | solution.py:22
  101.1 32.7 %collective-permute-start.9 = (bf16[256,64]{0,1:T(8,128)(2,1)}, bf16[256,64]{0,1:T(8,128)(2,1)}, u32[]{:S(2)}, u32[]{:S(2)}) collective-permute-start(bf16[256,64]{0,1:T(8,128)(2,1)} %maximum_select_fusion.24), channel_id=1, source_target_pairs={{2,0},{3,1},{4,2},{5,3},{6,4},{7,5},{8,6},{9,7},{10,8},{11,9},{12,... | collective-permute-start | bytes 98312 | tf_op jit(solution)/shard_map/ppermute | solution.py:22
  102.4 32.7 %collective-permute-start.7 = (bf16[256,64]{0,1:T(8,128)(2,1)}, bf16[256,64]{0,1:T(8,128)(2,1)}, u32[]{:S(2)}, u32[]{:S(2)}) collective-permute-start(bf16[256,64]{0,1:T(8,128)(2,1)} %maximum_select_fusion.24), channel_id=1, source_target_pairs={{0,2},{1,3},{2,4},{3,5},{4,6},{5,7},{6,8},{7,9},{8,10},{9,11},{10,... | collective-permute-start | bytes 98312 | tf_op jit(solution)/shard_map/ppermute | solution.py:22
  110.2 26.1 %collective-permute-start.5 = (bf16[256,64]{0,1:T(8,128)(2,1)}, bf16[256,64]{0,1:T(8,128)(2,1)}, u32[]{:S(2)}, u32[]{:S(2)}) collective-permute-start(bf16[256,64]{0,1:T(8,128)(2,1)} %maximum_select_fusion.24), channel_id=1, source_target_pairs={{0,4},{1,5},{2,6},{3,7},{4,8},{5,9},{6,10},{7,11},{8,12},{9,13},{1... | collective-permute-start | bytes 98312 | tf_op jit(solution)/shard_map/ppermute | solution.py:22
  132.0 39.3 %collective-permute-start.26 = (bf16[256,768]{1,0:T(8,128)(2,1)S(1)}, bf16[256,768]{1,0:T(8,128)(2,1)S(1)}, u32[]{:S(2)}, u32[]{:S(2)}) collective-permute-start(bf16[256,768]{1,0:T(8,128)(2,1)S(1)} %maximum_select_fusion.5), channel_id=1, source_target_pairs={{0,4},{1,5},{2,6},{3,7},{4,0},{5,1},{6,2},{7,3},{8,12},{9,13},{10,... | collective-permute-start | bytes 1179656 | tf_op jit(solution)/shard_map/ppermute | solution.py:16
  133.8 16.1 %collective-permute-start.75 = (bf16[1024,64]{1,0:T(8,128)(2,1)}, bf16[1024,64]{1,0:T(8,128)(2,1)S(1)}, u32[]{:S(2)}, u32[]{:S(2)}) collective-permute-start(bf16[1024,64]{1,0:T(8,128)(2,1)} %gather_fusion.4), channel_id=1, source_target_pairs={{4,0},{5,1},{6,2},{7,3},{8,4},{9,5},{10,6},{11,7},{12,8},{13,9},{1... | collective-permute-start | bytes 393224 | tf_op jit(solution)/shard_map/ppermute | solution.py:22
  135.1 19.4 %collective-permute-start.73 = (bf16[1024,64]{1,0:T(8,128)(2,1)}, bf16[1024,64]{1,0:T(8,128)(2,1)S(1)}, u32[]{:S(2)}, u32[]{:S(2)}) collective-permute-start(bf16[1024,64]{1,0:T(8,128)(2,1)} %gather_fusion.4), channel_id=1, source_target_pairs={{3,0},{4,1},{5,2},{6,3},{7,4},{8,5},{9,6},{10,7},{11,8},{12,9},{13... | collective-permute-start | bytes 393224 | tf_op jit(solution)/shard_map/ppermute | solution.py:22
  136.4 30.2 %collective-permute-start.71 = (bf16[1024,64]{1,0:T(8,128)(2,1)}, bf16[1024,64]{1,0:T(8,128)(2,1)S(1)}, u32[]{:S(2)}, u32[]{:S(2)}) collective-permute-start(bf16[1024,64]{1,0:T(8,128)(2,1)} %gather_fusion.4), channel_id=1, source_target_pairs={{2,0},{3,1},{4,2},{5,3},{6,4},{7,5},{8,6},{9,7},{10,8},{11,9},{12,... | collective-permute-start | bytes 393224 | tf_op jit(solution)/shard_map/ppermute | solution.py:22
  137.7 30.9 %collective-permute-start.69 = (bf16[1024,64]{1,0:T(8,128)(2,1)}, bf16[1024,64]{1,0:T(8,128)(2,1)S(1)}, u32[]{:S(2)}, u32[]{:S(2)}) collective-permute-start(bf16[1024,64]{1,0:T(8,128)(2,1)} %gather_fusion.4), channel_id=1, source_target_pairs={{1,0},{2,1},{3,2},{4,3},{5,4},{6,5},{7,6},{8,7},{9,8},{10,9},{11,1... | collective-permute-start | bytes 393224 | tf_op jit(solution)/shard_map/ppermute | solution.py:22
  149.9 25.3 %collective-permute-start.67 = (bf16[1024,64]{1,0:T(8,128)(2,1)}, bf16[1024,64]{1,0:T(8,128)(2,1)}, u32[]{:S(2)}, u32[]{:S(2)}) collective-permute-start(bf16[1024,64]{1,0:T(8,128)(2,1)} %gather_fusion.4), channel_id=1, source_target_pairs={{0,1},{1,2},{2,3},{3,4},{4,5},{5,6},{6,7},{7,8},{8,9},{9,10},{10,1... | collective-permute-start | bytes 393224 | tf_op jit(solution)/shard_map/ppermute | solution.py:22
  154.5 27.3 %collective-permute-start.65 = (bf16[1024,64]{1,0:T(8,128)(2,1)}, bf16[1024,64]{1,0:T(8,128)(2,1)}, u32[]{:S(2)}, u32[]{:S(2)}) collective-permute-start(bf16[1024,64]{1,0:T(8,128)(2,1)} %gather_fusion.4), channel_id=1, source_target_pairs={{0,2},{1,3},{2,4},{3,5},{4,6},{5,7},{6,8},{7,9},{8,10},{9,11},{10,... | collective-permute-start | bytes 393224 | tf_op jit(solution)/shard_map/ppermute | solution.py:22
  166.6 16.5 %collective-permute-start.63 = (bf16[1024,64]{1,0:T(8,128)(2,1)}, bf16[1024,64]{1,0:T(8,128)(2,1)}, u32[]{:S(2)}, u32[]{:S(2)}) collective-permute-start(bf16[1024,64]{1,0:T(8,128)(2,1)} %gather_fusion.4), channel_id=1, source_target_pairs={{0,3},{1,4},{2,5},{3,6},{4,7},{5,8},{6,9},{7,10},{8,11},{9,12},{10... | collective-permute-start | bytes 393224 | tf_op jit(solution)/shard_map/ppermute | solution.py:22
  168.6 20.0 %collective-permute-start.61 = (bf16[1024,64]{1,0:T(8,128)(2,1)}, bf16[1024,64]{1,0:T(8,128)(2,1)}, u32[]{:S(2)}, u32[]{:S(2)}) collective-permute-start(bf16[1024,64]{1,0:T(8,128)(2,1)} %gather_fusion.4), channel_id=1, source_target_pairs={{0,4},{1,5},{2,6},{3,7},{4,8},{5,9},{6,10},{7,11},{8,12},{9,13},{1... | collective-permute-start | bytes 393224 | tf_op jit(solution)/shard_map/ppermute | solution.py:22
  175.2 15.6 %collective-permute-start.25 = (bf16[256,64]{0,1:T(8,128)(2,1)}, bf16[256,64]{0,1:T(8,128)(2,1)S(1)}, u32[]{:S(2)}, u32[]{:S(2)}) collective-permute-start(bf16[256,64]{0,1:T(8,128)(2,1)} %copy-done.14), channel_id=1, source_target_pairs={{8,0},{9,1},{10,2},{11,3},{12,4},{13,5},{14,6},{15,7},{16,8},{17,9... | collective-permute-start | bytes 98312 | tf_op jit(solution)/shard_map/ppermute | solution.py:22
  183.1 19.2 %collective-permute-start.21 = (bf16[256,64]{0,1:T(8,128)(2,1)}, bf16[256,64]{0,1:T(8,128)(2,1)S(1)}, u32[]{:S(2)}, u32[]{:S(2)}) collective-permute-start(bf16[256,64]{0,1:T(8,128)(2,1)} %copy-done.14), channel_id=1, source_target_pairs={{0,4},{1,5},{2,6},{3,7},{4,8},{5,9},{6,10},{7,11},{8,12},{9,13},{1... | collective-permute-start | bytes 98312 | tf_op jit(solution)/shard_map/ppermute | solution.py:22
  190.8 168.8 %collective-permute-start.74 = (bf16[1024,768]{1,0:T(8,128)(2,1)S(1)}, bf16[1024,768]{1,0:T(8,128)(2,1)}, u32[]{:S(2)}, u32[]{:S(2)}) collective-permute-start(bf16[1024,768]{1,0:T(8,128)(2,1)S(1)} %copy-done.2), channel_id=1, source_target_pairs={{4,0},{5,1},{6,2},{7,3},{8,4},{9,5},{10,6},{11,7},{12,8},{13,9},{1... | collective-permute-start | bytes 4718600 | tf_op jit(solution)/shard_map/ppermute | solution.py:22
  192.1 170.8 %collective-permute-start.72 = (bf16[1024,768]{1,0:T(8,128)(2,1)S(1)}, bf16[1024,768]{1,0:T(8,128)(2,1)}, u32[]{:S(2)}, u32[]{:S(2)}) collective-permute-start(bf16[1024,768]{1,0:T(8,128)(2,1)S(1)} %copy-done.2), channel_id=1, source_target_pairs={{3,0},{4,1},{5,2},{6,3},{7,4},{8,5},{9,6},{10,7},{11,8},{12,9},{13... | collective-permute-start | bytes 4718600 | tf_op jit(solution)/shard_map/ppermute | solution.py:22
  203.7 67.7 %collective-permute-start.28 = (bf16[64,768]{1,0:T(8,128)(2,1)S(1)}, bf16[64,768]{1,0:T(8,128)(2,1)S(1)}, u32[]{:S(2)}, u32[]{:S(2)}) collective-permute-start(bf16[64,768]{1,0:T(8,128)(2,1)S(1)} %maximum_select_fusion.13), channel_id=1, source_target_pairs={{0,2},{1,3},{2,0},{3,1},{4,6},{5,7},{6,4},{7,5},{8,10},{9,11},{10,... | collective-permute-start | bytes 294920 | tf_op jit(solution)/shard_map/ppermute | solution.py:16
  203.8 68.5 %collective-permute-start.39 = (bf16[256,64]{1,0:T(8,128)(2,1)}, bf16[256,64]{1,0:T(8,128)(2,1)S(1)}, u32[]{:S(2)}, u32[]{:S(2)}) collective-permute-start(bf16[256,64]{1,0:T(8,128)(2,1)} %copy-done.13), channel_id=1, source_target_pairs={{8,0},{9,1},{10,2},{11,3},{12,4},{13,5},{14,6},{15,7},{16,8},{17,9... | collective-permute-start | bytes 98312 | tf_op jit(solution)/shard_map/ppermute | solution.py:22
  209.8 63.2 %collective-permute-start.37 = (bf16[256,64]{1,0:T(8,128)(2,1)}, bf16[256,64]{1,0:T(8,128)(2,1)S(1)}, u32[]{:S(2)}, u32[]{:S(2)}) collective-permute-start(bf16[256,64]{1,0:T(8,128)(2,1)} %copy-done.13), channel_id=1, source_target_pairs={{0,8},{1,9},{2,10},{3,11},{4,12},{5,13},{6,14},{7,15},{8,16},{9,17... | collective-permute-start | bytes 98312 | tf_op jit(solution)/shard_map/ppermute | solution.py:22
  272.4 26.6 %collective-permute-start.29 = (bf16[128,768]{1,0:T(8,128)(2,1)S(1)}, bf16[128,768]{1,0:T(8,128)(2,1)S(1)}, u32[]{:S(2)}, u32[]{:S(2)}) collective-permute-start(bf16[128,768]{1,0:T(8,128)(2,1)S(1)} %maximum_select_fusion.9), channel_id=1, source_target_pairs={{0,4},{1,5},{2,6},{3,7},{4,0},{5,1},{6,2},{7,3},{8,12},{9,13},{10,... | collective-permute-start | bytes 589832 | tf_op jit(solution)/shard_map/ppermute | solution.py:16
  277.7 22.6 %collective-permute-start.10 = (bf16[256,768]{1,0:T(8,128)(2,1)}, bf16[256,768]{1,0:T(8,128)(2,1)S(1)}, u32[]{:S(2)}, u32[]{:S(2)}) collective-permute-start(bf16[256,768]{1,0:T(8,128)(2,1)} %maximum_select_fusion.4), channel_id=1, source_target_pairs={{4,0},{5,1},{6,2},{7,3},{8,4},{9,5},{10,6},{11,7},{12,8},{13,9},{1... | collective-permute-start | bytes 1179656 | tf_op jit(solution)/shard_map/ppermute | solution.py:22
  298.9 86.0 %collective-permute-start.70 = (bf16[1024,768]{1,0:T(8,128)(2,1)S(1)}, bf16[1024,768]{1,0:T(8,128)(2,1)}, u32[]{:S(2)}, u32[]{:S(2)}) collective-permute-start(bf16[1024,768]{1,0:T(8,128)(2,1)S(1)} %copy-done.2), channel_id=1, source_target_pairs={{2,0},{3,1},{4,2},{5,3},{6,4},{7,5},{8,6},{9,7},{10,8},{11,9},{12,... | collective-permute-start | bytes 4718600 | tf_op jit(solution)/shard_map/ppermute | solution.py:22
  300.3 42.3 %collective-permute-start.42 = (bf16[256,768]{1,0:T(8,128)(2,1)S(1)}, bf16[256,768]{1,0:T(8,128)(2,1)S(1)}, u32[]{:S(2)}, u32[]{:S(2)}) collective-permute-start(bf16[256,768]{1,0:T(8,128)(2,1)S(1)} %maximum_select_fusion.6), channel_id=1, source_target_pairs={{0,8},{1,9},{2,10},{3,11},{4,12},{5,13},{6,14},{7,15},{8,0},{9,1},... | collective-permute-start | bytes 1179656 | tf_op jit(solution)/shard_map/ppermute | solution.py:16
  306.3 42.0 %collective-permute-start.6 = (bf16[256,768]{1,0:T(8,128)(2,1)}, bf16[256,768]{1,0:T(8,128)(2,1)}, u32[]{:S(2)}, u32[]{:S(2)}) collective-permute-start(bf16[256,768]{1,0:T(8,128)(2,1)} %maximum_select_fusion.4), channel_id=1, source_target_pairs={{0,2},{1,3},{2,4},{3,5},{4,6},{5,7},{6,8},{7,9},{8,10},{9,11},{10,... | collective-permute-start | bytes 1179656 | tf_op jit(solution)/shard_map/ppermute | solution.py:22
  342.7 16.8 %collective-permute-start.2 = (bf16[256,768]{1,0:T(8,128)(2,1)}, bf16[256,768]{1,0:T(8,128)(2,1)}, u32[]{:S(2)}, u32[]{:S(2)}) collective-permute-start(bf16[256,768]{1,0:T(8,128)(2,1)} %maximum_select_fusion.4), channel_id=1, source_target_pairs={{0,4},{1,5},{2,6},{3,7},{4,8},{5,9},{6,10},{7,11},{8,12},{9,13},{1... | collective-permute-start | bytes 1179656 | tf_op jit(solution)/shard_map/ppermute | solution.py:22
  356.4 108.0 %collective-permute-start.68 = (bf16[1024,768]{1,0:T(8,128)(2,1)S(1)}, bf16[1024,768]{1,0:T(8,128)(2,1)S(1)}, u32[]{:S(2)}, u32[]{:S(2)}) collective-permute-start(bf16[1024,768]{1,0:T(8,128)(2,1)S(1)} %copy-done.2), channel_id=1, source_target_pairs={{1,0},{2,1},{3,2},{4,3},{5,4},{6,5},{7,6},{8,7},{9,8},{10,9},{11,1... | collective-permute-start | bytes 4718600 | tf_op jit(solution)/shard_map/ppermute | solution.py:22
  359.6 123.5 %collective-permute-start.66 = (bf16[1024,768]{1,0:T(8,128)(2,1)S(1)}, bf16[1024,768]{1,0:T(8,128)(2,1)}, u32[]{:S(2)}, u32[]{:S(2)}) collective-permute-start(bf16[1024,768]{1,0:T(8,128)(2,1)S(1)} %copy-done.2), channel_id=1, source_target_pairs={{0,1},{1,2},{2,3},{3,4},{4,5},{5,6},{6,7},{7,8},{8,9},{9,10},{10,1... | collective-permute-start | bytes 4718600 | tf_op jit(solution)/shard_map/ppermute | solution.py:22
  362.9 121.5 %collective-permute-start.64 = (bf16[1024,768]{1,0:T(8,128)(2,1)S(1)}, bf16[1024,768]{1,0:T(8,128)(2,1)}, u32[]{:S(2)}, u32[]{:S(2)}) collective-permute-start(bf16[1024,768]{1,0:T(8,128)(2,1)S(1)} %copy-done.2), channel_id=1, source_target_pairs={{0,2},{1,3},{2,4},{3,5},{4,6},{5,7},{6,8},{7,9},{8,10},{9,11},{10,... | collective-permute-start | bytes 4718600 | tf_op jit(solution)/shard_map/ppermute | solution.py:22
  368.1 117.7 %collective-permute-start.62 = (bf16[1024,768]{1,0:T(8,128)(2,1)S(1)}, bf16[1024,768]{1,0:T(8,128)(2,1)}, u32[]{:S(2)}, u32[]{:S(2)}) collective-permute-start(bf16[1024,768]{1,0:T(8,128)(2,1)S(1)} %copy-done.2), channel_id=1, source_target_pairs={{0,3},{1,4},{2,5},{3,6},{4,7},{5,8},{6,9},{7,10},{8,11},{9,12},{10... | collective-permute-start | bytes 4718600 | tf_op jit(solution)/shard_map/ppermute | solution.py:22
  384.9 71.8 %collective-permute-start.45 = (bf16[64,768]{1,0:T(8,128)(2,1)S(1)}, bf16[64,768]{1,0:T(8,128)(2,1)S(1)}, u32[]{:S(2)}, u32[]{:S(2)}) collective-permute-start(bf16[64,768]{1,0:T(8,128)(2,1)S(1)} %maximum_select_fusion.14), channel_id=1, source_target_pairs={{0,4},{1,5},{2,6},{3,7},{4,0},{5,1},{6,2},{7,3},{8,12},{9,13},{10,... | collective-permute-start | bytes 294920 | tf_op jit(solution)/shard_map/ppermute | solution.py:16
  456.7 40.6 %collective-permute-start.60 = (bf16[1024,768]{1,0:T(8,128)(2,1)S(1)}, bf16[1024,768]{1,0:T(8,128)(2,1)}, u32[]{:S(2)}, u32[]{:S(2)}) collective-permute-start(bf16[1024,768]{1,0:T(8,128)(2,1)S(1)} %copy-done.2), channel_id=1, source_target_pairs={{0,4},{1,5},{2,6},{3,7},{4,8},{5,9},{6,10},{7,11},{8,12},{9,13},{1... | collective-permute-start | bytes 4718600 | tf_op jit(solution)/shard_map/ppermute | solution.py:22
  465.6 25.7 %collective-permute-start.46 = (bf16[128,768]{1,0:T(8,128)(2,1)}, bf16[128,768]{1,0:T(8,128)(2,1)}, u32[]{:S(2)}, u32[]{:S(2)}) collective-permute-start(bf16[128,768]{1,0:T(8,128)(2,1)} %maximum_select_fusion.10), channel_id=1, source_target_pairs={{0,8},{1,9},{2,10},{3,11},{4,12},{5,13},{6,14},{7,15},{8,0},{9,1},... | collective-permute-start | bytes 589832 | tf_op jit(solution)/shard_map/ppermute | solution.py:16
  485.7 31.4 %collective-permute-start.20 = (bf16[256,768]{1,0:T(8,128)(2,1)S(1)}, bf16[256,768]{1,0:T(8,128)(2,1)S(1)}, u32[]{:S(2)}, u32[]{:S(2)}) collective-permute-start(bf16[256,768]{1,0:T(8,128)(2,1)S(1)} %maximum_select_fusion.5), channel_id=1, source_target_pairs={{0,4},{1,5},{2,6},{3,7},{4,8},{5,9},{6,10},{7,11},{8,12},{9,13},{1... | collective-permute-start | bytes 1179656 | tf_op jit(solution)/shard_map/ppermute | solution.py:22
  491.3 27.9 %collective-permute-start.15 = (bf16[256,768]{1,0:T(8,128)(2,1)S(1)}, bf16[256,768]{1,0:T(8,128)(2,1)S(1)}, u32[]{:S(2)}, u32[]{:S(2)}) collective-permute-start(bf16[256,768]{1,0:T(8,128)(2,1)S(1)} %maximum_select_fusion.5), channel_id=1, source_target_pairs={{0,8},{1,9},{2,10},{3,11},{4,12},{5,13},{6,14},{7,15},{8,16},{9,17... | collective-permute-start | bytes 1179656 | tf_op jit(solution)/shard_map/ppermute | solution.py:22
  497.4 24.2 %collective-permute-start.40 = (bf16[256,768]{1,0:T(8,128)(2,1)}, bf16[256,768]{1,0:T(8,128)(2,1)}, u32[]{:S(2)}, u32[]{:S(2)}) collective-permute-start(bf16[256,768]{1,0:T(8,128)(2,1)} %copy-done.4), channel_id=1, source_target_pairs={{16,0},{17,1},{18,2},{19,3},{20,4},{21,5},{22,6},{23,7},{24,8},{25... | collective-permute-start | bytes 1179656 | tf_op jit(solution)/shard_map/ppermute | solution.py:22
  498.7 28.7 %collective-permute-start.38 = (bf16[256,768]{1,0:T(8,128)(2,1)}, bf16[256,768]{1,0:T(8,128)(2,1)}, u32[]{:S(2)}, u32[]{:S(2)}) collective-permute-start(bf16[256,768]{1,0:T(8,128)(2,1)} %copy-done.4), channel_id=1, source_target_pairs={{8,0},{9,1},{10,2},{11,3},{12,4},{13,5},{14,6},{15,7},{16,8},{17,9... | collective-permute-start | bytes 1179656 | tf_op jit(solution)/shard_map/ppermute | solution.py:22
  500.0 32.3 %collective-permute-start.36 = (bf16[256,768]{1,0:T(8,128)(2,1)}, bf16[256,768]{1,0:T(8,128)(2,1)}, u32[]{:S(2)}, u32[]{:S(2)}) collective-permute-start(bf16[256,768]{1,0:T(8,128)(2,1)} %copy-done.4), channel_id=1, source_target_pairs={{0,8},{1,9},{2,10},{3,11},{4,12},{5,13},{6,14},{7,15},{8,16},{9,17... | collective-permute-start | bytes 1179656 | tf_op jit(solution)/shard_map/ppermute | solution.py:22
  517.1 16.5 %collective-permute-start.30 = (bf16[256,768]{1,0:T(8,128)(2,1)}, bf16[256,768]{1,0:T(8,128)(2,1)}, u32[]{:S(2)}, u32[]{:S(2)}) collective-permute-start(bf16[256,768]{1,0:T(8,128)(2,1)} %copy-done.4), channel_id=1, source_target_pairs={{0,16},{1,17},{2,18},{3,19},{4,20},{5,21},{6,22},{7,23},{8,24},{9,... | collective-permute-start | bytes 1179656 | tf_op jit(solution)/shard_map/ppermute | solution.py:22
  519.9 19.9 %collective-permute-start.58 = (bf16[256,768]{1,0:T(8,128)(2,1)}, bf16[256,768]{1,0:T(8,128)(2,1)}, u32[]{:S(2)}, u32[]{:S(2)}) collective-permute-start(bf16[256,768]{1,0:T(8,128)(2,1)} %maximum_select_fusion.7), channel_id=1, source_target_pairs={{32,0},{33,1},{34,2},{35,3},{36,4},{37,5},{38,6},{39,7},{40,8},{41... | collective-permute-start | bytes 1179656 | tf_op jit(solution)/shard_map/ppermute | solution.py:22
  521.6 88.7 %collective-permute-start.55 = (bf16[256,64]{1,0:T(8,128)(2,1)}, bf16[256,64]{1,0:T(8,128)(2,1)}, u32[]{:S(2)}, u32[]{:S(2)}) collective-permute-start(bf16[256,64]{1,0:T(8,128)(2,1)} %maximum_select_fusion.22), channel_id=1, source_target_pairs={{0,16},{1,17},{2,18},{3,19},{4,20},{5,21},{6,22},{7,23},{8,24},{9,... | collective-permute-start | bytes 98312 | tf_op jit(solution)/shard_map/ppermute | solution.py:22
  527.4 83.6 %collective-permute-start.53 = (bf16[256,64]{1,0:T(8,128)(2,1)}, bf16[256,64]{1,0:T(8,128)(2,1)}, u32[]{:S(2)}, u32[]{:S(2)}) collective-permute-start(bf16[256,64]{1,0:T(8,128)(2,1)} %maximum_select_fusion.22), channel_id=1, source_target_pairs={{0,32},{1,33},{2,34},{3,35},{4,36},{5,37},{6,38},{7,39},{8,40},{9,... | collective-permute-start | bytes 98312 | tf_op jit(solution)/shard_map/ppermute | solution.py:22
  532.3 74.3 %collective-permute-start.56 = (bf16[256,768]{1,0:T(8,128)(2,1)}, bf16[256,768]{1,0:T(8,128)(2,1)}, u32[]{:S(2)}, u32[]{:S(2)}) collective-permute-start(bf16[256,768]{1,0:T(8,128)(2,1)} %maximum_select_fusion.7), channel_id=1, source_target_pairs={{16,0},{17,1},{18,2},{19,3},{20,4},{21,5},{22,6},{23,7},{24,8},{25... | collective-permute-start | bytes 1179656 | tf_op jit(solution)/shard_map/ppermute | solution.py:22
  533.6 76.7 %collective-permute-start.54 = (bf16[256,768]{1,0:T(8,128)(2,1)}, bf16[256,768]{1,0:T(8,128)(2,1)}, u32[]{:S(2)}, u32[]{:S(2)}) collective-permute-start(bf16[256,768]{1,0:T(8,128)(2,1)} %maximum_select_fusion.7), channel_id=1, source_target_pairs={{0,16},{1,17},{2,18},{3,19},{4,20},{5,21},{6,22},{7,23},{8,24},{9,... | collective-permute-start | bytes 1179656 | tf_op jit(solution)/shard_map/ppermute | solution.py:22
  539.8 71.2 %collective-permute-start.47 = (bf16[256,768]{1,0:T(8,128)(2,1)}, bf16[256,768]{1,0:T(8,128)(2,1)}, u32[]{:S(2)}, u32[]{:S(2)}) collective-permute-start(bf16[256,768]{1,0:T(8,128)(2,1)} %maximum_select_fusion.7), channel_id=1, source_target_pairs={{0,32},{1,33},{2,34},{3,35},{4,36},{5,37},{6,38},{7,39},{8,40},{9,... | collective-permute-start | bytes 1179656 | tf_op jit(solution)/shard_map/ppermute | solution.py:22
  619.2 83.1 %all-to-all-start.3 = ((f32[128,1,512]{2,1,0:T(1,128)}), f32[128,1,512]{2,1,0:T(1,128)S(1)}, u32[]{:S(2)}, u32[]{:S(2)}) async-start(f32[128,1,512]{2,1,0:T(1,128)} %reshape.602), calls=%async_computation.3 | async-start | bytes 524288 | tf_op jit(solution)/shard_map/all_to_all | solution.py:125
  (72 other events, 1550.3 us)
where the time goes:
time: 720 us; the launch traced here: 708 us
  starting transfers between devices  356 us (49%)
  waiting for transfers between devices  185 us (26%)
  local copies, waits for them, and re-layouts  57.3 us (8%)
  other arithmetic  46.5 us (6%)
  matrix products  45.8 us (6%)
  between operations  16.6 us (2%)
    ppermute x48, starting transfers between devices, from_behind(): return lax.ppermute(value, axis, pairs)  226 us
    ppermute x28, waiting for transfers between devices, from_partner(): return lax.ppermute(value, axis, pairs)  130 us
    all_to_all x1, starting transfers between devices, local(): lax.all_to_all(send_back, 'leaf', split_axis=0, concat_axis=0, tiled=True)  72.3 us
    dot_general x11, matrix products, evaluate(): return jnp.dot(kernel, operands[1], preferred_element_type=jnp.float32)  40.6 us
    ppermute x48, waiting for transfers between devices, from_behind(): return lax.ppermute(value, axis, pairs)  39.2 us
    ppermute x28, starting transfers between devices, from_partner(): return lax.ppermute(value, axis, pairs)  34.5 us
    reduce_sum x11, other arithmetic, row_offset(): squares = jnp.sum(jnp.square(block.astype(jnp.float32)), axis=1)  15.1 us
  transfers between devices with their start and end apart: 80, of which 24 were waited for; matrix products, arithmetic and copies ran while one was open for 17% of the time, Pallas kernels for 0%

commit v1 on v0

v1 whole, which is shorter than its diff:
```python
import math

import jax
import jax.numpy as jnp
from jax import lax
from jax.experimental import pallas as pl
from jax.experimental.pallas import tpu as pltpu
from jax.sharding import PartitionSpec as P

D = 768
W = 64
N = 1024
R = 256
LEAVES = 128
CHIPS = 64
GROUP = 16
PEER = N // LEAVES
MESSAGE = D + 128
MERGE = 240
PIECE = 2 * R + 128
F32 = jnp.float32
BF16 = jnp.bfloat16
SCALE = 1.0 / (1.75 * math.sqrt(D))
LOG2E = math.log2(math.e)
C_DOT = SCALE * LOG2E
C_SHIFT = 0.5 * SCALE * LOG2E
VMEM_LIMIT = 60 * 1024 * 1024
STEPS = (-2, -1, 1, 2)


def iota(shape, dim):
    return lax.broadcasted_iota(jnp.int32, shape, dim)


def one_hot(hit):
    return jnp.where(hit, 1.0, 0.0).astype(BF16)


def dot(a, b):
    return jnp.dot(a, b, preferred_element_type=F32)


def dot_nt(a, b):
    return lax.dot_general(a, b, (((1,), (1,)), ((), ())), preferred_element_type=F32)


def remote(src, dst, send, recv, device):
    return pltpu.make_async_remote_copy(
        src_ref=src,
        dst_ref=dst,
        send_sem=send,
        recv_sem=recv,
        device_id=(device,),
        device_id_type=pl.DeviceIdType.MESH,
    )


def greet(peers):
    barrier = pltpu.get_barrier_semaphore()
    for peer in peers:
        pl.semaphore_signal(
            barrier, inc=1, device_id=(peer,), device_id_type=pl.DeviceIdType.MESH
        )
    pl.semaphore_wait(barrier, len(peers))


def pack_kernel(slot_ref, pts_ref, tail_ref, piece_ref, send_ref, group_ref, send_sem, recv_sem):
    me = lax.axis_index("leaf")
    here = lax.rem(me, GROUP)
    base = me - here
    peers = [base + jnp.bitwise_xor(here, d) for d in range(1, GROUP)]
    greet(peers)
    copies = []
    for d in range(1, GROUP):
        first = 0 if d < 2 else 128 if d < 4 else 192 if d < 8 else 224
        rows = pl.ds(first, MERGE - first)
        copy = remote(
            piece_ref.at[rows],
            group_ref.at[here, rows],
            send_sem.at[d],
            recv_sem.at[d],
            peers[d - 1],
        )
        copy.start()
        copies.append(copy)
    group_ref[here] = piece_ref[...]

    row = slot_ref[...].astype(F32)
    col = jnp.transpose(jnp.broadcast_to(row, (8, N)))[:, 0:1]
    below = jnp.where(col < row, 1.0, 0.0)
    rank = jnp.sum(below, axis=0, keepdims=True).astype(jnp.int32)
    for i in range(4):
        rows = pl.ds(i * 256, 256)
        pick = one_hot(iota((256, N), 0) + i * 256 == rank)
        send_ref[rows, 0:D] = dot(pick, pts_ref[...]).astype(BF16)
        send_ref[rows, D:MESSAGE] = dot(pick, tail_ref[...]).astype(BF16)
    for copy in copies:
        copy.wait()


def unpack_kernel(slot_ref, home_ref, out_ref):
    row = slot_ref[...].astype(F32)
    col = jnp.transpose(jnp.broadcast_to(row, (8, N)))[:, 0:1]
    below = jnp.where(row < col, 1.0, 0.0)
    rank = jnp.sum(below, axis=1, keepdims=True).astype(jnp.int32)
    for i in range(4):
        pick = one_hot(iota((256, N), 1) == rank[i * 256 : (i + 1) * 256])
        both = dot(pick, home_ref[...])
        out_ref[pl.ds(i * 256, 256), :] = both[:, 0:W] + both[:, W : 2 * W]


class Copies:
    def __init__(self, send_sem, recv_sem):
        self.send_sem, self.recv_sem, self.all = send_sem, recv_sem, []

    def start(self, src, dst, device, recv=None):
        i = len(self.all)
        recv = i if recv is None else recv
        copy = remote(src, dst, self.send_sem.at[i], self.recv_sem.at[recv], device)
        copy.start()
        self.all.append(copy)
        return copy


COPIES = 80


def pick_lane(row, column):
    return jnp.sum(
        jnp.where(iota(row.shape, 1) == column, row, 0.0), axis=1, keepdims=True
    )


def tree_kernel(
    got, interp, skel_row, skel_col, mask_rows, group,
    out,
    xw, xv, mp, mw, mv, yp, yw, yv, rp, rw, rv,
    b1, b2, b3, b4, n4, far,
    pick_t, acol, ycol,
    xwt, ywt, mwt, rwx, rwy, xwm, mwm,
    acc_x, acc_y, acc_xt, acc_mt, acc_rt,
    ret_m, ret_y, ret_r, in_m, in_y, in_r,
    send_sem, recv_sem,
):
    me = lax.axis_index("leaf")
    chip = me // 2
    core = lax.rem(me, 2)
    mate = me + 1 - 2 * core

    def at(offset, which=None):
        other = lax.rem(chip + offset + CHIPS, CHIPS)
        return other * 2 + (core if which is None else which)

    right, left = at(1), at(-1)
    greet(
        [mate, at(1, 1 - core), at(-1, 1 - core)]
        + [at(o) for o in (1, -1, 2, -2, 4, -4, 8, -8, 16, -16)]
    )
    copies = Copies(send_sem, recv_sem)
    pts = got.at[:, pl.ds(0, D)]
    quarter = [pl.ds(256 * i, 256) for i in range(4)]

    mate_p = copies.start(pts, mp, mate)
    to_right, to_left = [], []

    def send_quarter(i):
        src = got.at[quarter[i], pl.ds(0, D)]
        to_left.append(copies.start(src, rp.at[core, quarter[i]], left))
        to_right.append(copies.start(src, yp.at[quarter[i]], right))

    send_quarter(0)

    lane = iota((1, 128), 1)
    for q in quarter:
        x = got[q, 0:D].astype(F32)
        acol[q, :] = (jnp.sum(x * x, axis=1, keepdims=True) - float(D)) * C_SHIFT
    a = acol[...]
    a_wide = jnp.broadcast_to(a, (N, 128))
    xv[...] = jnp.where(
        iota((8, N), 0) == 0, jnp.transpose(a_wide)[0:8], mask_rows[...]
    )
    tail = got[:, D:MESSAGE].astype(F32)
    place = (tail[:, W : W + 1] * 32.0 + tail[:, W + 1 : W + 2]).astype(jnp.int32)
    tail_t = jnp.transpose(tail)
    place_row = (tail_t[W : W + 1] * 32.0 + tail_t[W + 1 : W + 2]).astype(jnp.int32)
    high = a_wide.astype(BF16).astype(F32)
    middle = (a_wide - high).astype(BF16).astype(F32)
    low = a_wide - high - middle
    aux = jnp.where(lane == W, high, jnp.where(lane == W + 1, middle, low))
    aux = jnp.where((lane >= W) & (lane < W + 3), aux, 0.0).astype(BF16)
    pick_t[...] = one_hot(place == skel_row[...])
    own_pick = one_hot(skel_col[...] == place_row)
    tree_w = dot(one_hot(iota((N, N), 0) == place_row), got[:, D:MESSAGE]).astype(BF16)
    skel_w = dot(interp[...], tree_w)
    b1[core, :, 0:D] = dot(own_pick, got[:, 0:D]).astype(BF16)
    b1[core, :, D:MESSAGE] = jnp.where(lane < W, skel_w, dot(own_pick, aux)).astype(BF16)
    level0 = copies.start(b1.at[core], b1.at[core], mate)

    def merge(level, children, store):
        rows = R >> level
        first = R - 2 * rows
        here = lax.rem(me, GROUP)
        base = here - lax.rem(here, 1 << level)
        pieces = jnp.concatenate(
            [group[base + p, first : first + rows, :] for p in range(1 << level)], axis=0
        )
        index = pieces[:, 2 * R : 2 * R + 1].astype(F32) * 32.0
        index = index + pieces[:, 2 * R + 1 : 2 * R + 2].astype(F32)
        chosen = one_hot(index.astype(jnp.int32) == iota((R, 2 * R), 1))
        both = children[...].reshape(2 * R, MESSAGE)
        new_w = dot(pieces[:, 0 : 2 * R], both[:, D:MESSAGE])
        new = dot(chosen, both)
        new_tail = jnp.where(lane < W, new_w, new[:, D:MESSAGE]).astype(BF16)
        store[:, 0:D] = new[:, 0:D].astype(BF16)
        store[:, D:MESSAGE] = new_tail
        return chosen, new_tail

    half = pl.ds(pl.multiple_of(core * 128, 128), 128)

    def send_far(slot, offset, node):
        return [
            copies.start(node.at[half], far.at[slot + i, half], at(-step * offset))
            for i, step in enumerate(STEPS)
        ]

    def pass_on(copy, ref):
        copy.wait_recv()
        return copies.start(ref, ref, mate)

    x_t = jnp.transpose(tail)

    def block(tp, ta, tw_t, sp, sa, sw, acc_t, acc_s):
        k = dot_nt(tp, sp) * C_DOT
        k = jnp.exp2(k - ta - sa).astype(BF16)
        if acc_t is not None:
            acc_t[...] += dot(k, sw)
        if acc_s is not None:
            acc_s[...] += dot(tw_t, k)

    acc_x[...] = jnp.zeros_like(acc_x)
    acc_y[...] = jnp.zeros_like(acc_y)
    acc_xt[...] = jnp.zeros_like(acc_xt)
    acc_mt[...] = jnp.zeros_like(acc_mt)
    acc_rt[...] = jnp.zeros_like(acc_rt)
    mwt[...] = jnp.where(iota((128, 1), 0) < W, x_t, 0.0).astype(BF16)
    xwm[...] = jnp.where(lane < W, tail, 0.0).astype(BF16)

    def own_block(i):
        for j in range(i, 4):
            block(
                got[quarter[i], 0:D], acol[quarter[i], :], mwt[:, quarter[i]],
                got[quarter[j], 0:D], xv[0:1, quarter[j]], xwm[quarter[j], :],
                acc_x.at[quarter[i]], acc_xt.at[:, quarter[j]] if j > i else None,
            )

    own_block(0)

    level0.wait_recv()
    side2 = lax.rem(chip, 2)
    chosen, tail1 = merge(1, b1, b2.at[side2])
    level1 = copies.start(b2.at[side2, half], b2.at[side2, half], jnp.bitwise_xor(chip, 1) * 2 + core)
    send_quarter(1)
    mine = jnp.where(core == 0, chosen[:, 0:R].astype(F32), chosen[:, R : 2 * R].astype(F32))
    placed = dot_nt(pick_t[...], mine.astype(BF16)).astype(BF16)
    spread = pltpu.roll(dot(placed, tail1), W, 1)
    x_w = jnp.where(lane < W, tail, spread)
    xw[...] = x_w.astype(BF16)
    wv = []
    for src, dm, dl, dr in ((xw, mw, rw.at[core], yw), (xv, mv, rv.at[core], yv)):
        wv.append(
            (copies.start(src, dm, mate), copies.start(src, dl, left), copies.start(src, dr, right))
        )

    own_block(1)

    level1.wait_recv()
    other2 = b2.at[1 - side2, half]
    shared = copies.start(other2, other2, mate)
    own_block(2)
    own_block(3)
    shared.wait_recv()
    side3 = lax.rem(chip // 2, 2)
    merge(2, b2, b3.at[side3])
    level2 = copies.start(b3.at[side3, half], b3.at[side3, half], jnp.bitwise_xor(chip, 2) * 2 + core)
    far_copies = send_far(0, 2, b3.at[side3])
    send_quarter(2)

    mate_p.wait_recv()
    wv[0][0].wait_recv()
    wv[1][0].wait_recv()
    near_mate = pick_lane(xv[1:2, :], jnp.where(core == 0, 4, 3))
    mwm[...] = jnp.where(lane < W, mw[...].astype(F32) * near_mate, 0.0).astype(BF16)
    mwt[...] = (mwt[...].astype(F32) * near_mate).astype(BF16)

    def mate_block(h):
        for i in range(2):
            mine = pl.ds(h * 512 + i * 256, 256)
            theirs = pl.ds(pl.multiple_of(jnp.bitwise_xor(core, h) * 512, 512), 512)
            block(
                got[mine, 0:D], acol[mine, :], mwt[:, mine],
                mp[theirs, :], mv[0:1, theirs], mwm[theirs, :],
                acc_x.at[mine], acc_mt.at[:, theirs],
            )

    mate_block(0)
    level2.wait_recv()
    other3 = b3.at[1 - side3, half]
    shared = copies.start(other3, other3, mate)
    mate_block(1)
    ret_m[...] = acc_mt[0:W, :]
    back_m = copies.start(ret_m, in_m, mate)
    shared.wait_recv()
    side4 = lax.rem(chip // 4, 2)
    merge(3, b3, b4.at[side4])
    level3 = copies.start(b4.at[side4, half], b4.at[side4, half], jnp.bitwise_xor(chip, 4) * 2 + core)
    far_copies += send_far(4, 4, b4.at[side4])
    send_quarter(3)

    passed_w = [pass_on(wv[0][1], rw.at[core]), pass_on(wv[1][1], rv.at[core])]
    passed_p = [pass_on(to_left[0], rp.at[core, quarter[0]])]
    level3.wait_recv()
    other4 = b4.at[1 - side4, half]
    shared = copies.start(other4, other4, mate)
    wv[0][2].wait_recv()
    wv[1][2].wait_recv()
    y_row = jnp.broadcast_to(yv[0:1, :], (8, N))
    ycol[...] = jnp.transpose(y_row)[:, 0:1]
    y_w = yw[...].astype(F32)
    y_t = jnp.transpose(y_w)
    x_t = jnp.transpose(xw[...].astype(F32))
    shared.wait_recv()
    merge(4, b4, n4)
    far_copies += send_far(8, 8, n4)
    for copy in passed_w:
        copy.wait_recv()
    low_lane = lane < W
    low_row = iota((128, 1), 0) < W
    x_mask, y_mask = xv[1:2, :], yv[1:2, :]
    for j in range(2):
        r_mask = rv[j, 1:2, :]
        r_w = rw[j].astype(F32)
        step = 2 + j - core
        near = pick_lane(x_mask, step + 3)
        rwx[j] = (r_w * jnp.where(low_lane, near, pick_lane(x_mask, 8 + 2))).astype(BF16)
        xwt[j] = (x_t * jnp.where(low_row, near, pick_lane(r_mask, 8 + 1))).astype(BF16)
        step = 4 + j - core
        near = jnp.where(step <= 4, pick_lane(y_mask, step + 3), 0.0)
        rwy[j] = (r_w * jnp.where(low_lane, near, pick_lane(y_mask, 8 + 3))).astype(BF16)
        ywt[j] = (y_t * jnp.where(low_row, near, pick_lane(r_mask, 8 + 0))).astype(BF16)

    def near_quarter(i, tp, ta, tw_t, sw, acc):
        @pl.loop(0, 4)
        def _(t):
            rows = pl.ds(pl.multiple_of(t * 256, 256), 256)
            for j in range(2):
                block(
                    tp[rows, 0:D], ta[rows, :], tw_t[j, :, rows],
                    rp[j, quarter[i], :], rv[j, 0:1, quarter[i]], sw[j, quarter[i], :],
                    acc.at[rows], acc_rt.at[j, :, quarter[i]],
                )

    for i in range(4):
        passed_p[i].wait_recv()
        if i < 3:
            passed_p.append(pass_on(to_left[i + 1], rp.at[core, quarter[i + 1]]))
        near_quarter(i, got, acol, xwt, rwx, acc_x)
    for copy in to_right:
        copy.wait_recv()
    far_passed = []
    for i in range(4):
        for slot in range(3 * i, 3 * i + 3):
            far_passed.append(pass_on(far_copies[slot], far.at[slot, half]))
        near_quarter(i, yp, ycol, ywt, rwy, acc_y)
    y_sum = acc_y[:, 0:W] + acc_y[:, W : 2 * W]
    ret_y[...] = jnp.transpose(jnp.concatenate([y_sum, y_sum], axis=1))[0:W]
    ret_r[...] = acc_rt[:, 0:W, :] + acc_rt[:, W : 2 * W, :]
    back_y = copies.start(ret_y, in_y, left)
    for j in range(2):
        copies.start(ret_r.at[j], in_r.at[core], at(1, j), COPIES - 2 + core)

    for copy in far_passed:
        copy.wait_recv()

    @pl.loop(0, 12)
    def _(slot):
        mask = pick_lane(x_mask, 12 + slot)
        f_tail = far[slot, :, D:MESSAGE].astype(F32)
        f_w = jnp.where(low_lane, f_tail * mask, 0.0).astype(BF16)
        f_t = jnp.transpose(f_tail)
        f_a = f_t[W : W + 1] + f_t[W + 1 : W + 2] + f_t[W + 2 : W + 3]
        f_p = far[slot, :, 0:D]
        for t in range(4):
            block(
                got[quarter[t], 0:D], acol[quarter[t], :], None,
                f_p, f_a, f_w, acc_x.at[quarter[t]], None,
            )

    back_m.wait_recv()
    back_y.wait_recv()
    for j in range(2):
        remote(
            ret_r.at[j], in_r.at[j], send_sem.at[COPIES - 1], recv_sem.at[COPIES - 2 + j], left
        ).wait_recv()
    total = acc_xt[0:W, :] + in_m[...] + in_y[...] + in_r[0] + in_r[1]
    total = jnp.transpose(jnp.concatenate([total, total], axis=0))
    x_sum = acc_x[...]
    total = total + x_sum + pltpu.roll(x_sum, W, 1)
    high = total.astype(BF16).astype(F32)
    out[...] = jnp.where(lane < W, high, total - high).astype(BF16)
    for copy in copies.all:
        copy.wait_send()


def vmem(*shape, dtype=BF16):
    return pltpu.VMEM(shape, dtype)


def in_vmem(count):
    return [pl.BlockSpec(memory_space=pltpu.VMEM)] * count


def local(
    points, weights, tree_slot, leaf_interp, skel_leaf, merge_interp, merge_index, near_mask, far_mask
):
    slot_row = tree_slot.reshape(1, N)
    place = lax.rem(tree_slot, N)
    tail = jnp.concatenate(
        [
            weights,
            (place // 32).astype(BF16)[:, None],
            lax.rem(place, 32).astype(BF16)[:, None],
            jnp.zeros((N, 128 - W - 2), BF16),
        ],
        axis=1,
    )
    index = merge_index[0]
    piece = jnp.concatenate(
        [
            merge_interp[0],
            (index // 32).astype(BF16)[:, None],
            lax.rem(index, 32).astype(BF16)[:, None],
            jnp.zeros((MERGE, 126), BF16),
        ],
        axis=1,
    )
    mask_row = jnp.concatenate(
        [near_mask.reshape(1, 8), far_mask.reshape(1, 16)], axis=1
    ).astype(F32)
    mask_rows = jnp.pad(mask_row, ((1, 6), (0, N - 24)))
    send, group = pl.pallas_call(
        pack_kernel,
        out_shape=[
            jax.ShapeDtypeStruct((N, MESSAGE), BF16),
            jax.ShapeDtypeStruct((GROUP, MERGE, PIECE), BF16),
        ],
        in_specs=in_vmem(4),
        out_specs=in_vmem(2),
        scratch_shapes=[pltpu.SemaphoreType.DMA((GROUP,)), pltpu.SemaphoreType.DMA((GROUP,))],
        compiler_params=pltpu.CompilerParams(
            collective_id=0, has_side_effects=True, vmem_limit_bytes=VMEM_LIMIT
        ),
        name="pack",
    )(slot_row, points, tail, piece)
    got = lax.all_to_all(
        send.reshape(LEAVES, PEER, MESSAGE), "leaf", split_axis=0, concat_axis=0, tiled=True
    ).reshape(N, MESSAGE)
    sums = pl.pallas_call(
        tree_kernel,
        out_shape=jax.ShapeDtypeStruct((N, 128), BF16),
        in_specs=in_vmem(6),
        out_specs=pl.BlockSpec(memory_space=pltpu.VMEM),
        scratch_shapes=[
            vmem(N, 128), vmem(8, N, dtype=F32),
            vmem(N, D), vmem(N, 128), vmem(8, N, dtype=F32),
            vmem(N, D), vmem(N, 128), vmem(8, N, dtype=F32),
            vmem(2, N, D), vmem(2, N, 128), vmem(2, 8, N, dtype=F32),
            vmem(2, R, MESSAGE), vmem(2, R, MESSAGE), vmem(2, R, MESSAGE), vmem(2, R, MESSAGE),
            vmem(R, MESSAGE), vmem(12, R, MESSAGE),
            vmem(N, R), vmem(N, 1, dtype=F32), vmem(N, 1, dtype=F32),
            vmem(2, 128, N), vmem(2, 128, N), vmem(128, N),
            vmem(2, N, 128), vmem(2, N, 128), vmem(N, 128), vmem(N, 128),
            vmem(N, 128, dtype=F32), vmem(N, 128, dtype=F32),
            vmem(128, N, dtype=F32), vmem(128, N, dtype=F32), vmem(2, 128, N, dtype=F32),
            vmem(W, N, dtype=F32), vmem(W, N, dtype=F32), vmem(2, W, N, dtype=F32),
            vmem(W, N, dtype=F32), vmem(W, N, dtype=F32), vmem(2, W, N, dtype=F32),
            pltpu.SemaphoreType.DMA((COPIES,)), pltpu.SemaphoreType.DMA((COPIES,)),
        ],
        compiler_params=pltpu.CompilerParams(
            collective_id=1, has_side_effects=True, vmem_limit_bytes=VMEM_LIMIT
        ),
        name="tree",
    )(got, leaf_interp[0], skel_leaf, skel_leaf.reshape(R, 1), mask_rows, group)
    home = lax.all_to_all(
        sums.reshape(LEAVES, PEER, 128), "leaf", split_axis=0, concat_axis=0, tiled=True
    ).reshape(N, 128)
    return pl.pallas_call(
        unpack_kernel,
        out_shape=jax.ShapeDtypeStruct((N, W), F32),
        in_specs=in_vmem(2),
        out_specs=pl.BlockSpec(memory_space=pltpu.VMEM),
        compiler_params=pltpu.CompilerParams(vmem_limit_bytes=VMEM_LIMIT),
        name="unpack",
    )(slot_row, home)


def solution(mesh):
    placed = (
        P("leaf", None),
        P("leaf", None),
        P("leaf"),
        P("leaf", None, None),
        P("leaf", None),
        P("leaf", None, None),
        P("leaf", None),
        P("leaf", None),
        P("leaf", None, None),
    )
    return jax.shard_map(
        local, mesh=mesh, in_specs=placed, out_specs=P("leaf", None), check_vma=False
    )
```

time: 720 us -> 228 us (0.32); the launches traced: 708 us -> 228 us
  starting transfers between devices: 356 us -> 7.86 us
  waiting for transfers between devices: 185 us -> 26 us
  Pallas kernels: 0 us -> 153 us
  local copies, waits for them, and re-layouts: 57.3 us -> 7.19 us
  matrix products: 45.8 us -> 0 us
  other arithmetic: 46.5 us -> 2.68 us
  blocking collectives: 0 us -> 31.4 us
  between operations: 16.6 us -> 0.11 us
    ppermute x76 -> x0, starting transfers between devices: 261 us -> none  [the longest x48 226 us: from_behind(): return lax.ppermute(value, axis, pairs)]
    ppermute x76 -> x0, waiting for transfers between devices: 169 us -> none  [the longest x28 130 us: from_partner(): return lax.ppermute(value, axis, pairs)]
    pallas_call x0 -> x3, Pallas kernels: none -> 153 us  [the longest x1 126 us: local(): pl.pallas_call(tree_kernel, out_shape=jax.ShapeDtypeStruct((N, 128), BF16...]
    all_to_all x4 -> x1, starting transfers between devices: 95.3 us -> 7.86 us  [local(): lax.all_to_all(send.reshape(LEAVES, PEER, MESSAGE), 'leaf', split_axis=0,...]
    dot_general x16 -> x0, matrix products: 45.8 us -> none  [the longest x11 40.6 us: evaluate(): return jnp.dot(kernel, operands[1], preferred_element_type=jnp.float32)]
    gather x13 -> x0, local copies, waits for them, and re-layouts: 38.6 us -> none  [the longest x4 6.52 us: local(): part_pts = both_pts[piece_index]]
    all_to_all x0 -> x1, blocking collectives: none -> 31.4 us  [local(): lax.all_to_all(sums.reshape(LEAVES, PEER, 128), 'leaf', split_axis=0, con...]
    reduce_sum x11 -> x0, other arithmetic: 15.1 us -> none  [row_offset(): squares = jnp.sum(jnp.square(block.astype(jnp.float32)), axis=1)]
  transfers between devices with their start and end apart: 80 -> 1, of which waited for: 24 -> 1; matrix products, arithmetic and copies ran while one was open for 17% -> 1% of each run, Pallas kernels for 0% -> 0%
where the time goes in v1:
time: 228 us
  Pallas kernels  153 us (67%)
  blocking collectives  31.4 us (14%)
  waiting for transfers between devices  26 us (11%)
  starting transfers between devices  7.86 us (3%)
  local copies, waits for them, and re-layouts  7.19 us (3%)
  other arithmetic  2.68 us (1%)
    pallas_call x1, Pallas kernels, local(): pl.pallas_call(tree_kernel, out_shape=jax.ShapeDtypeStruct((N, 128), BF16...  126 us
    all_to_all x1, blocking collectives, local(): lax.all_to_all(sums.reshape(LEAVES, PEER, 128), 'leaf', split_axis=0, con...  31.4 us
    all_to_all x1, waiting for transfers between devices, local(): lax.all_to_all(send.reshape(LEAVES, PEER, MESSAGE), 'leaf', split_axis=0,...  26 us
    pallas_call x1, Pallas kernels, local(): pl.pallas_call(pack_kernel, out_shape=[jax.ShapeDtypeStruct((N, MESSAGE),...  23.4 us
    all_to_all x1, starting transfers between devices, local(): lax.all_to_all(send.reshape(LEAVES, PEER, MESSAGE), 'leaf', split_axis=0,...  7.86 us
  transfers between devices with their start and end apart: 1, of which 1 were waited for; matrix products, arithmetic and copies ran while one was open for 1% of the time, Pallas kernels for 0%

profile of v1, /device:TPU:1, one launch (start us, length us, event | category | flops | bytes accessed | tf_op | source)
XLA Modules:
  0.0 227.9 jit_solution(18166974701984559957)
XLA Ops:
  0.0 0.0 copy-start.1
  0.0 0.7 fusion.4
  0.7 0.2 broadcast_in_dim.18
  1.0 0.2 broadcast_in_dim.19
  1.2 1.1 copy.12
  2.2 0.8 copy.15
  3.1 0.1 fusion
  3.2 0.1 pad.14.clone
  3.2 0.1 pad.10.clone
  3.3 1.0 maximum_maximum_fusion.1.tail_ref
  4.3 0.0 copy-done.1
  4.3 0.8 maximum_maximum_fusion.piece_ref
  5.1 23.4 %pack.1 = (bf16[1024,896]{1,0:T(8,128)(2,1)}, bf16[16,240,640]{2,1,0:T(8,128)(2,1)}) custom-call(s32[1,1024]{1,0:T(1,128)} %bitcast.15, bf16[1024,768]{1,0:T(8,128)(2,1)} %pts_ref.1, bf16[1024,128]{1,0:T(8,128)(2,1)} %maximum_maximum_fusion.1.tail_ref, bf16[240,640]{1,0:T(8,128)(2,1)} %maximum_maximum_fusion.piece_ref), custom_call_target="tpu_custom_call" | custom-call | tf_op jit(solution)/shard_map/pack/pallas_call | solution.py:450
  28.5 0.0 copy-start.2
  28.5 0.0 copy-start.3
  28.5 0.0 copy-start.4
  28.5 7.9 %all-to-all-start = ((bf16[128,8,896]{2,1,0:T(8,128)(2,1)}), bf16[128,8,896]{2,1,0:T(8,128)(2,1)S(1)}, u32[]{:S(2)}, u32[]{:S(2)}) async-start(bf16[128,8,896]{2,1,0:T(8,128)(2,1)} %bitcast.10), calls=%async_computation | async-start | bytes 3670016 | tf_op jit(solution)/shard_map/all_to_all | solution.py:464
  36.4 0.0 copy-done.2
  36.4 0.8 copy.19.skel_col
  37.2 0.0 copy-done.3
  37.2 0.1 concatenate.21
  37.3 0.0 copy-done.4
  37.3 0.1 add_convert_fusion
  37.4 0.6 pad.4.mask_rows
  38.0 26.0 %all-to-all-done = bf16[128,8,896]{2,1,0:T(8,128)(2,1)S(1)} async-done(((bf16[128,8,896]{2,1,0:T(8,128)(2,1)}), bf16[128,8,896]{2,1,0:T(8,128)(2,1)S(1)}, u32[]{:S(2)}, u32[]{:S(2)}) %all-to-all-start) | async-done | bytes 1835040 | tf_op jit(solution)/shard_map/all_to_all | solution.py:464
  64.0 0.0 copy-start
  64.0 1.3 copy-done
  65.3 125.6 %tree.1 = bf16[1024,128]{1,0:T(8,128)(2,1)} custom-call(bf16[1024,896]{1,0:T(8,128)(2,1)} %bitcast.9, bf16[256,1024]{1,0:T(8,128)(2,1)} %bitcast.13, s32[1,256]{1,0:T(1,128)} %skel_row.1, s32[256,1]{1,0:T(8,128)} %copy.19.skel_col, f32[8,1024]{1,0:T(8,128)} %pad.4.mask_rows, bf16[16,240,640]{2,1,0:T(8,128)(2,1)} %get-tuple-element.8.group), custom_call_target="tpu_custom_call" | custom-call | tf_op jit(solution)/shard_map/tree/pallas_call | solution.py:467
  191.0 31.4 %all_to_all.10 = bf16[128,8,128]{2,1,0:T(8,128)(2,1)} all-to-all(bf16[128,8,128]{2,1,0:T(8,128)(2,1)} %bitcast.11), channel_id=1, replica_groups=mesh['leaf'=128] {'leaf'}, dimensions={0} | all-to-all | bytes 524288 | tf_op jit(solution)/shard_map/all_to_all | solution.py:493
  222.3 3.6 %unpack.1 = f32[1024,64]{1,0:T(8,128)} custom-call(s32[1,1024]{1,0:T(1,128)} %bitcast.16, bf16[1024,128]{1,0:T(8,128)(2,1)} %bitcast.12), custom_call_target="tpu_custom_call" | custom-call | tf_op jit(solution)/shard_map/unpack/pallas_call | solution.py:496
  226.0 1.9 copy.20
  (2 shorter events, 0.0 us)
Async XLA Ops:
  0.0 4.3 %copy-start.1 = (bf16[1,240,512]{2,1,0:T(8,128)(2,1)S(1)}, bf16[1,240,512]{2,1,0:T(8,128)(2,1)}, u32[]{:S(2)}) copy-start(bf16[1,240,512]{2,1,0:T(8,128)(2,1)} %param.14) | copy-start | bytes 737284
  28.5 7.9 %copy-start.2 = (s32[1,256]{1,0:T(1,128)S(1)}, s32[1,256]{1,0:T(1,128)}, u32[]{:S(2)}) copy-start(s32[1,256]{1,0:T(1,128)} %skel_row.1) | copy-start | bytes 3076
  28.5 8.7 %copy-start.3 = (s32[1,4,4]{2,1,0:T(4,128)S(1)}, s32[1,4,4]{2,1,0:T(4,128)}, u32[]{:S(2)}) copy-start(s32[1,4,4]{2,1,0:T(4,128)} %param.17) | copy-start | bytes 196
  28.5 8.8 %copy-start.4 = (s32[1,8]{1,0:T(1,128)S(1)}, s32[1,8]{1,0:T(1,128)}, u32[]{:S(2)}) copy-start(s32[1,8]{1,0:T(1,128)} %param.16) | copy-start | bytes 100
  28.5 35.5 %all-to-all-start = ((bf16[128,8,896]{2,1,0:T(8,128)(2,1)}), bf16[128,8,896]{2,1,0:T(8,128)(2,1)S(1)}, u32[]{:S(2)}, u32[]{:S(2)}) async-start(bf16[128,8,896]{2,1,0:T(8,128)(2,1)} %bitcast.10), calls=%async_computation | async-start | bytes 3670016 | tf_op jit(solution)/shard_map/all_to_all | solution.py:464
  64.0 1.3 copy-start

commit v2 on v1

v2 whole, which is shorter than its diff:
```python
import math

import jax
import jax.numpy as jnp
from jax import lax
from jax.experimental import pallas as pl
from jax.experimental.pallas import tpu as pltpu
from jax.sharding import PartitionSpec as P

D = 768
W = 64
N = 1024
R = 256
LEAVES = 128
CHIPS = 64
GROUP = 16
PEER = N // LEAVES
MESSAGE = D + 128
MERGE = 240
F32 = jnp.float32
BF16 = jnp.bfloat16
SCALE = 1.0 / (1.75 * math.sqrt(D))
LOG2E = math.log2(math.e)
C_DOT = SCALE * LOG2E
C_SHIFT = 0.5 * SCALE * LOG2E
VMEM_LIMIT = 60 * 1024 * 1024


def iota(shape, dim):
    return lax.broadcasted_iota(jnp.int32, shape, dim)


def one_hot(hit):
    return jnp.where(hit, 1.0, 0.0).astype(BF16)


def dot(a, b):
    return jnp.dot(a, b, preferred_element_type=F32)


def dot_nt(a, b):
    return lax.dot_general(a, b, (((1,), (1,)), ((), ())), preferred_element_type=F32)


def remote(src, dst, send, recv, device):
    return pltpu.make_async_remote_copy(
        src_ref=src,
        dst_ref=dst,
        send_sem=send,
        recv_sem=recv,
        device_id=(device,),
        device_id_type=pl.DeviceIdType.MESH,
    )


class Copies:
    def __init__(self, send_sem, recv_sem):
        self.send_sem, self.recv_sem, self.all = send_sem, recv_sem, []

    def start(self, src, dst, device, recv=None):
        i = len(self.all)
        recv = i if recv is None else recv
        copy = remote(src, dst, self.send_sem.at[i], self.recv_sem.at[recv], device)
        copy.start()
        self.all.append(copy)
        return copy


COPIES = 160


def pick_lane(row, column):
    return jnp.sum(
        jnp.where(iota(row.shape, 1) == column, row, 0.0), axis=1, keepdims=True
    )


def column_of(row):
    return jnp.transpose(jnp.broadcast_to(row, (8, row.shape[1])))[:, 0:1]


def tree_kernel(
    slot, weights_t, points, interp, skel_row, merge_w, merge_i, near_mask, far_mask,
    out,
    send, came, got, tail_s, index, lines,
    xw, xv, mp, mw, mv, yp, yw, yv, rp, rw, rv,
    b1, b2, b3, b4, n4, w0, w1, w2, w3, w4, far,
    pick_t, acol, ycol,
    xwt, ywt, mwt, rwx, rwy, xwm, mwm,
    acc_x, acc_y, acc_xt, acc_mt, acc_rt,
    ret_m, ret_y, ret_r, in_m, in_y, in_r,
    back, home,
    send_sem, recv_sem, all_sem,
):
    me = lax.axis_index("leaf")
    chip = me // 2
    core = lax.rem(me, 2)
    mate = me + 1 - 2 * core
    here = lax.rem(me, GROUP)

    def at(offset, which=None):
        other = lax.rem(chip + offset + CHIPS, CHIPS)
        return other * 2 + (core if which is None else which)

    barrier = pltpu.get_barrier_semaphore()

    @pl.loop(1, LEAVES)
    def _(d):
        pl.semaphore_signal(
            barrier,
            inc=1,
            device_id=(lax.rem(me + d, LEAVES),),
            device_id_type=pl.DeviceIdType.MESH,
        )

    right, left = at(1), at(-1)
    copies = Copies(send_sem, recv_sem)
    quarter = [pl.ds(256 * i, 256) for i in range(4)]
    lane = iota((1, 128), 1)

    row = slot[...].astype(F32)
    rank = jnp.sum(jnp.where(column_of(row) < row, 1.0, 0.0), axis=0, keepdims=True)
    rank = rank.astype(jnp.int32)
    spot = jnp.bitwise_and(slot[...], N - 1)
    tail_s[...] = jnp.zeros_like(tail_s)
    tail_s[0:W, :] = weights_t[...].astype(F32)
    tail_s[W : W + 1, :] = jnp.right_shift(spot, 5).astype(F32)
    tail_s[W + 1 : W + 2, :] = jnp.bitwise_and(spot, 31).astype(F32)
    tail_in = jnp.transpose(tail_s[...]).astype(BF16)
    for i in range(4):
        pick = one_hot(iota((256, N), 0) + i * 256 == rank)
        rows = pl.ds(i * 32, 32)
        send[rows, :, 0:D] = dot(pick, points[...]).reshape(32, PEER, D).astype(BF16)
        send[rows, :, D:MESSAGE] = dot(pick, tail_in).reshape(32, PEER, 128).astype(BF16)
    lines[...] = jnp.zeros_like(lines)
    lines[0:1, 0:MERGE] = merge_i[...].astype(F32)
    merge_c = jnp.transpose(lines[...])[0:MERGE, 0:1].astype(jnp.int32)
    merge_h = jnp.right_shift(merge_c, 5).astype(F32)
    merge_l = jnp.bitwise_and(merge_c, 31).astype(F32)
    index[here] = jnp.where(lane == 0, merge_h, jnp.where(lane == 1, merge_l, 0.0)).astype(BF16)

    pl.semaphore_wait(barrier, LEAVES - 1)

    @pl.loop(1, LEAVES)
    def _(d):
        other = lax.rem(me + d, LEAVES)
        remote(send.at[other], came.at[me], all_sem.at[0], all_sem.at[1], other).start()

    indices = []
    for d in range(1, GROUP):
        first = 0 if d < 2 else 128 if d < 4 else 192 if d < 8 else 224
        rows = pl.ds(first, MERGE - first)
        indices.append(
            copies.start(index.at[here, rows], index.at[here, rows], me - here + jnp.bitwise_xor(here, d))
        )
    came[me] = send[me]
    skel_col = column_of(skel_row[...].astype(F32)).astype(jnp.int32)
    mask_row = jnp.zeros((1, N), F32)
    wide = iota((1, N), 1)
    for i in range(8):
        mask_row = jnp.where(wide == i, near_mask[0, i].astype(F32), mask_row)
    for i in range(16):
        mask_row = jnp.where(wide == 8 + i, far_mask[0, i // 4, i % 4].astype(F32), mask_row)
    for acc in (acc_x, acc_y, acc_xt, acc_mt, acc_rt):
        acc[...] = jnp.zeros_like(acc)
    everyone = remote(
        send.at[pl.ds(0, LEAVES - 1)], came.at[pl.ds(0, LEAVES - 1)], all_sem.at[0], all_sem.at[1], mate
    )
    everyone.wait_recv()

    for i in range(4):
        part = came[pl.ds(32 * i, 32)].astype(F32).reshape(256, MESSAGE)
        got[quarter[i], :] = part.astype(BF16)
        x = part[:, 0:D]
        acol[quarter[i], :] = (jnp.sum(x * x, axis=1, keepdims=True) - float(D)) * C_SHIFT
    to_right, to_left = [], []

    def send_quarter(i):
        src = got.at[quarter[i], pl.ds(0, D)]
        to_left.append(copies.start(src, rp.at[core, quarter[i]], left))
        to_right.append(copies.start(src, yp.at[quarter[i]], right))

    send_quarter(0)
    a_wide = jnp.broadcast_to(acol[...], (N, 128))
    xv[...] = jnp.where(iota((8, N), 0) == 0, jnp.transpose(a_wide)[0:8], mask_row)
    tail = got[:, D:MESSAGE].astype(F32)
    place = (tail[:, W : W + 1] * 32.0 + tail[:, W + 1 : W + 2]).astype(jnp.int32)
    tail_t = jnp.transpose(tail)
    place_row = (tail_t[W : W + 1] * 32.0 + tail_t[W + 1 : W + 2]).astype(jnp.int32)
    high = a_wide.astype(BF16).astype(F32)
    middle = (a_wide - high).astype(BF16).astype(F32)
    low = a_wide - high - middle
    aux = jnp.where(lane == W, high, jnp.where(lane == W + 1, middle, low))
    aux = jnp.where((lane >= W) & (lane < W + 3), aux, 0.0).astype(BF16)
    own_pick = one_hot(skel_col == place_row)
    b1[core, :, 0:D] = dot(own_pick, got[:, 0:D]).astype(BF16)
    b1[core, :, D:MESSAGE] = dot(own_pick, aux).astype(BF16)
    level0 = copies.start(b1.at[core], b1.at[core], mate)
    tree_w = dot(one_hot(iota((N, N), 0) == place_row), got[:, D:MESSAGE]).astype(BF16)
    own_w = pl.ds(pl.multiple_of(core * R, R), R)
    w0[own_w, :] = dot(interp[...], tree_w).astype(BF16)
    weight0 = copies.start(w0.at[own_w], w0.at[own_w], mate)
    mate_p = copies.start(got.at[:, pl.ds(0, D)], mp, mate)
    pick_t[...] = one_hot(place == skel_row[...])
    mwt[...] = jnp.where(iota((128, 1), 0) < W, tail_t, 0.0).astype(BF16)
    xwm[...] = jnp.where(lane < W, tail, 0.0).astype(BF16)

    def merge_points(level, children, store):
        rows = R >> level
        first = R - 2 * rows
        base = here - lax.rem(here, 1 << level)
        pieces = jnp.concatenate(
            [index[base + p, first : first + rows, :] for p in range(1 << level)], axis=0
        ).astype(F32)
        index_k = (pieces[:, 0:1] * 32.0 + pieces[:, 1:2]).astype(jnp.int32)
        chosen = one_hot(index_k == iota((R, 2 * R), 1))
        both = children[...].reshape(2 * R, MESSAGE)
        store[...] = dot(chosen, both).astype(BF16)
        return chosen

    def merge_weights(level, children, store):
        rows = R >> level
        first = R - 2 * rows
        span = min(2 << level, GROUP)
        mine = pl.ds(pl.multiple_of(lax.rem(here, span) * rows, rows), rows)
        store[mine, :] = dot(merge_w[first : first + rows, :], children[...]).astype(BF16)
        return [
            copies.start(
                store.at[mine], store.at[mine], me - here + jnp.bitwise_xor(here, d)
            )
            for d in range(1, span)
        ]

    def arrive(group):
        for copy in group:
            copy.wait_recv()

    half = pl.ds(pl.multiple_of(core * 128, 128), 128)
    even = lax.rem(chip, 2) == 0
    even4 = lax.rem(chip // 4, 2) == 0
    third, first = jnp.where(even, 3, 1), jnp.where(even, 1, 3)
    third4, first4 = jnp.where(even4, 12, 4), jnp.where(even4, 4, 12)
    targets = (
        (4, third, -first, -4),
        (8, 4, -4, -8),
        (16, third4, -first4, -16),
    )

    def send_far(level, node):
        return [
            copies.start(
                node.at[half, pl.ds(0, D)], far.at[4 * level + i, half, pl.ds(0, D)], at(targets[level][i])
            )
            for i in range(4)
        ]

    def send_far_tail(level, node):
        return [
            copies.start(
                node.at[:, pl.ds(D, 128)], far.at[4 * level + i, :, pl.ds(D, 128)], at(targets[level][i])
            )
            for i in range(4)
        ]

    def pass_on(copy, ref):
        copy.wait_recv()
        return copies.start(ref, ref, mate)

    def pass_far(slot):
        return pass_on(far_points[slot], far.at[slot, half, pl.ds(0, D)])

    def block(tp, ta, tw_t, sp, sa, sw, acc_t, acc_s):
        k = dot_nt(tp, sp) * C_DOT
        k = jnp.exp2(k - ta - sa).astype(BF16)
        if acc_t is not None:
            acc_t[...] += dot(k, sw)
        if acc_s is not None:
            acc_s[...] += dot(tw_t, k)

    def own_block(i):
        for j in range(i, 4):
            block(
                got[quarter[i], 0:D], acol[quarter[i], :], mwt[:, quarter[i]],
                got[quarter[j], 0:D], xv[0:1, quarter[j]], xwm[quarter[j], :],
                acc_x.at[quarter[i]], acc_xt.at[:, quarter[j]] if j > i else None,
            )

    own_block(0)

    arrive(indices)
    level0.wait_recv()
    side2 = lax.rem(chip, 2)
    chosen = merge_points(1, b1, b2.at[side2])
    level1 = copies.start(
        b2.at[side2, half], b2.at[side2, half], jnp.bitwise_xor(chip, 1) * 2 + core
    )
    weight0.wait_recv()
    weight1 = merge_weights(1, w0, w1)
    send_quarter(1)
    own_block(1)
    arrive(weight1)
    mine = jnp.where(core == 0, chosen[:, 0:R].astype(F32), chosen[:, R : 2 * R].astype(F32))
    placed = dot_nt(pick_t[...], mine.astype(BF16)).astype(BF16)
    tail1 = w1[pl.ds(pl.multiple_of(side2 * R, R), R), :]
    spread = pltpu.roll(dot(placed, tail1), W, 1)
    x_w = jnp.where(lane < W, tail, spread)
    xw[...] = x_w.astype(BF16)
    wv = []
    for src, dm, dl, dr in ((xw, mw, rw.at[core], yw), (xv, mv, rv.at[core], yv)):
        wv.append(
            (copies.start(src, dm, mate), copies.start(src, dl, left), copies.start(src, dr, right))
        )
    weight2 = merge_weights(2, w1, w2)

    level1.wait_recv()
    other2 = b2.at[1 - side2, half]
    shared = copies.start(other2, other2, mate)
    own_block(2)
    own_block(3)
    shared.wait_recv()
    side3 = lax.rem(chip // 2, 2)
    merge_points(2, b2, b3.at[side3])
    level2 = copies.start(
        b3.at[side3, half], b3.at[side3, half], jnp.bitwise_xor(chip, 3) * 2 + core
    )
    far_points = send_far(0, b3.at[side3])
    arrive(weight2)
    weight3 = merge_weights(3, w2, w3)
    send_quarter(2)

    mate_p.wait_recv()
    wv[0][0].wait_recv()
    wv[1][0].wait_recv()
    near_mate = pick_lane(xv[1:2, :], jnp.where(core == 0, 4, 3))
    mwm[...] = jnp.where(lane < W, mw[...].astype(F32) * near_mate, 0.0).astype(BF16)
    mwt[...] = (mwt[...].astype(F32) * near_mate).astype(BF16)

    def mate_block(h):
        for i in range(2):
            mine = pl.ds(h * 512 + i * 256, 256)
            theirs = pl.ds(pl.multiple_of(jnp.bitwise_xor(core, h) * 512, 512), 512)
            block(
                got[mine, 0:D], acol[mine, :], mwt[:, mine],
                mp[theirs, :], mv[0:1, theirs], mwm[theirs, :],
                acc_x.at[mine], acc_mt.at[:, theirs],
            )

    mate_block(0)
    passed_w = [pass_on(wv[0][1], rw.at[core]), pass_on(wv[1][1], rv.at[core])]
    passed_p = [pass_on(to_left[0], rp.at[core, quarter[0]])]
    mate_block(1)
    ret_m[...] = acc_mt[0:W, :]
    back_m = copies.start(ret_m, in_m, mate)
    level2.wait_recv()
    other3 = b3.at[1 - side3, half]
    shared = copies.start(other3, other3, mate)

    wv[0][2].wait_recv()
    wv[1][2].wait_recv()
    y_row = jnp.broadcast_to(yv[0:1, :], (8, N))
    ycol[...] = jnp.transpose(y_row)[:, 0:1]
    y_w = yw[...].astype(F32)
    y_t = jnp.transpose(y_w)
    x_t = jnp.transpose(xw[...].astype(F32))
    arrive(passed_w)
    low_lane = lane < W
    low_row = iota((128, 1), 0) < W
    x_mask, y_mask = xv[1:2, :], yv[1:2, :]
    for j in range(2):
        r_mask = rv[j, 1:2, :]
        r_w = rw[j].astype(F32)
        step = 2 + j - core
        near = pick_lane(x_mask, step + 3)
        rwx[j] = (r_w * jnp.where(low_lane, near, pick_lane(x_mask, 8 + 2))).astype(BF16)
        xwt[j] = (x_t * jnp.where(low_row, near, pick_lane(r_mask, 8 + 1))).astype(BF16)
        step = 4 + j - core
        near = jnp.where(step <= 4, pick_lane(y_mask, step + 3), 0.0)
        rwy[j] = (r_w * jnp.where(low_lane, near, pick_lane(y_mask, 8 + 3))).astype(BF16)
        ywt[j] = (y_t * jnp.where(low_row, near, pick_lane(r_mask, 8 + 0))).astype(BF16)

    def near_block(i, rows, tp, ta, tw_t, sw, acc):
        for j in range(2):
            block(
                tp[rows, 0:D], ta[rows, :], tw_t[j, :, rows],
                rp[j, i, :], rv[j, 0:1, i], sw[j, i, :],
                acc.at[rows], acc_rt.at[j, :, i],
            )

    def x_quarter(i):
        arrive([passed_p[i]])

        @pl.loop(0, 4)
        def _(t):
            rows = pl.ds(pl.multiple_of(t * 256, 256), 256)
            near_block(quarter[i], rows, got, acol, xwt, rwx, acc_x)

    def y_quarter(i):
        to_right[i].wait_recv()

        @pl.loop(0, i + 1)
        def _(t):
            rows = pl.ds(pl.multiple_of(t * 256, 256), 256)
            near_block(quarter[i], rows, yp, ycol, ywt, rwy, acc_y)

        @pl.loop(0, i)
        def _(t):
            rows = pl.ds(pl.multiple_of(t * 256, 256), 256)
            near_block(rows, quarter[i], yp, ycol, ywt, rwy, acc_y)

    x_quarter(0)
    shared.wait_recv()
    side4 = lax.rem(chip // 4, 2)
    merge_points(3, b3, b4.at[side4])
    level3 = copies.start(
        b4.at[side4, half], b4.at[side4, half], jnp.bitwise_xor(chip, 4) * 2 + core
    )
    far_points += send_far(1, b4.at[side4])
    arrive(weight3)
    weight4 = merge_weights(4, w3, w4)
    send_quarter(3)

    def with_weights(node, weights):
        node[:, D:MESSAGE] = jnp.where(
            lane < W, weights.astype(F32), node[:, D:MESSAGE].astype(F32)
        ).astype(BF16)

    y_quarter(0)
    passed_p.append(pass_on(to_left[1], rp.at[core, quarter[1]]))
    level3.wait_recv()
    other4 = b4.at[1 - side4, half]
    shared = copies.start(other4, other4, mate)
    x_quarter(1)
    shared.wait_recv()
    merge_points(4, b4, n4)
    far_points += send_far(2, n4)
    arrive(weight4)
    level1.wait_send()
    level2.wait_send()
    level3.wait_send()
    far_tails = []
    for level, node, weights in (
        (0, b3.at[side3], w2[pl.ds(pl.multiple_of(side3 * R, R), R), :]),
        (1, b4.at[side4], w3[pl.ds(pl.multiple_of(side4 * R, R), R), :]),
        (2, n4, w4[...]),
    ):
        with_weights(node, weights)
        far_tails += send_far_tail(level, node)
    y_quarter(1)
    passed_p.append(pass_on(to_left[2], rp.at[core, quarter[2]]))
    far_passed = [pass_far(slot) for slot in range(4)]
    x_quarter(2)
    y_quarter(2)
    passed_p.append(pass_on(to_left[3], rp.at[core, quarter[3]]))
    far_passed += [pass_far(slot) for slot in range(4, 8)]
    x_quarter(3)
    y_quarter(3)
    far_passed += [pass_far(slot) for slot in range(8, 12)]
    y_sum = acc_y[:, 0:W] + acc_y[:, W : 2 * W]
    ret_y[...] = jnp.transpose(jnp.concatenate([y_sum, y_sum], axis=1))[0:W]
    ret_r[...] = acc_rt[:, 0:W, :] + acc_rt[:, W : 2 * W, :]
    back_y = copies.start(ret_y, in_y, left)
    for j in range(2):
        copies.start(ret_r.at[j], in_r.at[core], at(1, j), COPIES - 2 + core)

    arrive(far_tails)
    arrive(far_passed)

    @pl.loop(0, 12)
    def _(slot):
        mask = pick_lane(x_mask, 12 + slot)
        f_tail = far[slot, :, D:MESSAGE].astype(F32)
        f_w = jnp.where(low_lane, f_tail * mask, 0.0).astype(BF16)
        f_t = jnp.transpose(f_tail)
        f_a = f_t[W : W + 1] + f_t[W + 1 : W + 2] + f_t[W + 2 : W + 3]
        f_p = far[slot, :, 0:D]
        for t in range(4):
            block(
                got[quarter[t], 0:D], acol[quarter[t], :], None,
                f_p, f_a, f_w, acc_x.at[quarter[t]], None,
            )

    back_m.wait_recv()
    back_y.wait_recv()
    for j in range(2):
        remote(
            ret_r.at[j], in_r.at[j], send_sem.at[COPIES - 1], recv_sem.at[COPIES - 2 + j], left
        ).wait_recv()
    total = acc_xt[0:W, :] + in_m[...] + in_y[...] + in_r[0] + in_r[1]
    total = jnp.transpose(jnp.concatenate([total, total], axis=0))
    x_sum = acc_x[...]
    total = total + x_sum + pltpu.roll(x_sum, W, 1)
    high = total.astype(BF16).astype(F32)
    total = jnp.where(lane < W, high, total - high)
    back[...] = total.reshape(LEAVES, PEER, 128).astype(BF16)

    @pl.loop(1, LEAVES)
    def _(d):
        other = lax.rem(me + d, LEAVES)
        remote(back.at[other], home.at[me], all_sem.at[2], all_sem.at[3], other).start()

    home[me] = back[me]
    everyone.wait_send()
    for copy in copies.all:
        if not any(copy is sent for sent in (level1, level2, level3)):
            copy.wait_send()
    row = slot[...].astype(F32)
    rank = jnp.sum(jnp.where(column_of(row) < row, 1.0, 0.0), axis=0, keepdims=True)
    rank = rank.astype(jnp.int32)
    returned = remote(
        back.at[pl.ds(0, LEAVES - 1)], home.at[pl.ds(0, LEAVES - 1)], all_sem.at[2], all_sem.at[3], mate
    )
    returned.wait_recv()
    home_t = jnp.transpose(home[...].astype(F32).reshape(N, 128)).astype(BF16)
    for i in range(4):
        pick = one_hot(iota((N, 256), 0) == rank[:, 256 * i : 256 * (i + 1)])
        both = dot(home_t, pick)
        out[:, quarter[i]] = both[0:W] + both[W : 2 * W]
    returned.wait_send()


def vmem(*shape, dtype=BF16):
    return pltpu.VMEM(shape, dtype)


def local(
    points, weights, tree_slot, leaf_interp, skel_leaf, merge_interp, merge_index, near_mask, far_mask
):
    in_vmem = pl.BlockSpec(memory_space=pltpu.VMEM)
    in_smem = pl.BlockSpec(memory_space=pltpu.SMEM)
    sums = pl.pallas_call(
        tree_kernel,
        out_shape=jax.ShapeDtypeStruct((W, N), F32),
        in_specs=[in_vmem] * 7 + [in_smem] * 2,
        out_specs=in_vmem,
        scratch_shapes=[
            vmem(LEAVES, PEER, MESSAGE), vmem(LEAVES, PEER, MESSAGE), vmem(N, MESSAGE),
            vmem(128, N, dtype=F32), vmem(GROUP, MERGE, 128), vmem(8, 256, dtype=F32),
            vmem(N, 128), vmem(8, N, dtype=F32),
            vmem(N, D), vmem(N, 128), vmem(8, N, dtype=F32),
            vmem(N, D), vmem(N, 128), vmem(8, N, dtype=F32),
            vmem(2, N, D), vmem(2, N, 128), vmem(2, 8, N, dtype=F32),
            vmem(2, R, MESSAGE), vmem(2, R, MESSAGE), vmem(2, R, MESSAGE), vmem(2, R, MESSAGE),
            vmem(R, MESSAGE),
            vmem(2 * R, 128), vmem(2 * R, 128), vmem(2 * R, 128), vmem(2 * R, 128), vmem(R, 128),
            vmem(12, R, MESSAGE),
            vmem(N, R), vmem(N, 1, dtype=F32), vmem(N, 1, dtype=F32),
            vmem(2, 128, N), vmem(2, 128, N), vmem(128, N),
            vmem(2, N, 128), vmem(2, N, 128), vmem(N, 128), vmem(N, 128),
            vmem(N, 128, dtype=F32), vmem(N, 128, dtype=F32),
            vmem(128, N, dtype=F32), vmem(128, N, dtype=F32), vmem(2, 128, N, dtype=F32),
            vmem(W, N, dtype=F32), vmem(W, N, dtype=F32), vmem(2, W, N, dtype=F32),
            vmem(W, N, dtype=F32), vmem(W, N, dtype=F32), vmem(2, W, N, dtype=F32),
            vmem(LEAVES, PEER, 128), vmem(LEAVES, PEER, 128),
            pltpu.SemaphoreType.DMA((COPIES,)), pltpu.SemaphoreType.DMA((COPIES,)),
            pltpu.SemaphoreType.DMA((4,)),
        ],
        compiler_params=pltpu.CompilerParams(
            collective_id=0, has_side_effects=True, vmem_limit_bytes=VMEM_LIMIT
        ),
        name="tree",
    )(
        tree_slot.reshape(1, N), weights.T, points, leaf_interp[0], skel_leaf, merge_interp[0],
        merge_index, near_mask, far_mask,
    )
    return sums.T


def solution(mesh):
    placed = (
        P("leaf", None),
        P("leaf", None),
        P("leaf"),
        P("leaf", None, None),
        P("leaf", None),
        P("leaf", None, None),
        P("leaf", None),
        P("leaf", None),
        P("leaf", None, None),
    )
    return jax.shard_map(
        local, mesh=mesh, in_specs=placed, out_specs=P("leaf", None), check_vma=False
    )
```

time: 228 us -> 181 us (0.79)
  blocking collectives: 31.4 us -> 0 us
  Pallas kernels: 153 us -> 179 us
  waiting for transfers between devices: 26 us -> 0 us
  starting transfers between devices: 7.86 us -> 0 us
  local copies, waits for them, and re-layouts: 7.19 us -> 1.67 us
  other arithmetic: 2.68 us -> 0 us
    all_to_all x1 -> x0, blocking collectives: 31.4 us -> none  [local(): lax.all_to_all(sums.reshape(LEAVES, PEER, 128), 'leaf', split_axis=0, con...]
    pallas_call x3 -> x1, Pallas kernels: 153 us -> 179 us  [local(): pl.pallas_call(tree_kernel, out_shape=jax.ShapeDtypeStruct((W, N), F32),...]
    all_to_all x1 -> x0, waiting for transfers between devices: 26 us -> none  [local(): lax.all_to_all(send.reshape(LEAVES, PEER, MESSAGE), 'leaf', split_axis=0,...]
    all_to_all x1 -> x0, starting transfers between devices: 7.86 us -> none  [local(): lax.all_to_all(send.reshape(LEAVES, PEER, MESSAGE), 'leaf', split_axis=0,...]
  transfers between devices with their start and end apart: 1 -> 0, of which waited for: 1 -> 0; matrix products, arithmetic and copies ran while one was open for 1% -> 0% of each run, Pallas kernels for 0% -> 0%
where the time goes in v2:
time: 181 us
  Pallas kernels  179 us (99%)
    pallas_call x1, Pallas kernels, local(): pl.pallas_call(tree_kernel, out_shape=jax.ShapeDtypeStruct((W, N), F32),...  179 us

profile of v2, /device:TPU:1, one launch (start us, length us, event | category | flops | bytes accessed | tf_op | source)
XLA Modules:
  0.0 181.1 jit_solution(13328885760351537440)
XLA Ops:
  0.0 179.4 %tree.1 = f32[64,1024]{1,0:T(8,128)} custom-call(s32[1,1024]{1,0:T(1,128)} %bitcast.9, bf16[64,1024]{1,0:T(8,128)(2,1)} %bitcast.8, bf16[1024,768]{1,0:T(8,128)(2,1)} %points.1, bf16[256,1024]{1,0:T(8,128)(2,1)} %bitcast.6, s32[1,256]{1,0:T(1,128)} %skel_row.1, bf16[240,512]{1,0:T(8,128)(2,1)} %bitcast.7, s32[1,240]{1,0:T(1,128)} %merge_i.1, ...), custom_call_target="tpu_custom_call" | custom-call | tf_op jit(solution)/shard_map/tree/pallas_call | solution.py:530
  179.4 1.7 copy.11

commit v3 on v2

--- a/solution.py
+++ b/solution.py
@@ -15,6 +15,7 @@
 CHIPS = 64
 GROUP = 16
 PEER = N // LEAVES
+STRIDE = 37
 MESSAGE = D + 128
 MERGE = 240
 F32 = jnp.float32
@@ -143,7 +144,7 @@
 
     @pl.loop(1, LEAVES)
     def _(d):
-        other = lax.rem(me + d, LEAVES)
+        other = lax.rem(me + d * STRIDE, LEAVES)
         remote(send.at[other], came.at[me], all_sem.at[0], all_sem.at[1], other).start()
 
     indices = []
@@ -296,7 +297,6 @@
     )
     weight0.wait_recv()
     weight1 = merge_weights(1, w0, w1)
-    send_quarter(1)
     own_block(1)
     arrive(weight1)
     mine = jnp.where(core == 0, chosen[:, 0:R].astype(F32), chosen[:, R : 2 * R].astype(F32))
@@ -326,7 +326,7 @@
     far_points = send_far(0, b3.at[side3])
     arrive(weight2)
     weight3 = merge_weights(3, w2, w3)
-    send_quarter(2)
+    send_quarter(1)
 
     mate_p.wait_recv()
     wv[0][0].wait_recv()
@@ -388,26 +388,35 @@
 
     def x_quarter(i):
         arrive([passed_p[i]])
-
-        @pl.loop(0, 4)
-        def _(t):
-            rows = pl.ds(pl.multiple_of(t * 256, 256), 256)
+        for rows in quarter:
             near_block(quarter[i], rows, got, acol, xwt, rwx, acc_x)
 
     def y_quarter(i):
         to_right[i].wait_recv()
-
-        @pl.loop(0, i + 1)
-        def _(t):
-            rows = pl.ds(pl.multiple_of(t * 256, 256), 256)
+        for rows in quarter[: i + 1]:
             near_block(quarter[i], rows, yp, ycol, ywt, rwy, acc_y)
-
-        @pl.loop(0, i)
-        def _(t):
-            rows = pl.ds(pl.multiple_of(t * 256, 256), 256)
+        for rows in quarter[:i]:
             near_block(rows, quarter[i], yp, ycol, ywt, rwy, acc_y)
 
-    x_quarter(0)
+    def far_level(level):
+        arrive(far_tails[4 * level : 4 * level + 4])
+        arrive(far_passed[4 * level : 4 * level + 4])
+        for first_slot in (4 * level, 4 * level + 2):
+            f_p, f_a, f_w = [], [], []
+            for slot in (first_slot, first_slot + 1):
+                f_tail = far[slot, :, D:MESSAGE].astype(F32)
+                f_w.append(jnp.where(low_lane, f_tail * pick_lane(x_mask, 12 + slot), 0.0))
+                f_t = jnp.transpose(f_tail)
+                f_a.append(f_t[W : W + 1] + f_t[W + 1 : W + 2] + f_t[W + 2 : W + 3])
+                f_p.append(far[slot, :, 0:D])
+            f_p = jnp.concatenate(f_p, axis=0)
+            f_a = jnp.concatenate(f_a, axis=1)
+            f_w = jnp.concatenate(f_w, axis=0).astype(BF16)
+            for rows in quarter:
+                block(
+                    got[rows, 0:D], acol[rows, :], None, f_p, f_a, f_w, acc_x.at[rows], None
+                )
+
     shared.wait_recv()
     side4 = lax.rem(chip // 4, 2)
     merge_points(3, b3, b4.at[side4])
@@ -417,19 +426,20 @@
     far_points += send_far(1, b4.at[side4])
     arrive(weight3)
     weight4 = merge_weights(4, w3, w4)
+    send_quarter(2)
     send_quarter(3)
+    x_quarter(0)
 
     def with_weights(node, weights):
         node[:, D:MESSAGE] = jnp.where(
             lane < W, weights.astype(F32), node[:, D:MESSAGE].astype(F32)
         ).astype(BF16)
 
-    y_quarter(0)
-    passed_p.append(pass_on(to_left[1], rp.at[core, quarter[1]]))
     level3.wait_recv()
     other4 = b4.at[1 - side4, half]
     shared = copies.start(other4, other4, mate)
-    x_quarter(1)
+    passed_p.append(pass_on(to_left[1], rp.at[core, quarter[1]]))
+    y_quarter(0)
     shared.wait_recv()
     merge_points(4, b4, n4)
     far_points += send_far(2, n4)
@@ -445,47 +455,35 @@
     ):
         with_weights(node, weights)
         far_tails += send_far_tail(level, node)
+    x_quarter(1)
+    passed_p.append(pass_on(to_left[2], rp.at[core, quarter[2]]))
     y_quarter(1)
-    passed_p.append(pass_on(to_left[2], rp.at[core, quarter[2]]))
+    x_quarter(2)
     far_passed = [pass_far(slot) for slot in range(4)]
-    x_quarter(2)
     y_quarter(2)
+    far_level(0)
     passed_p.append(pass_on(to_left[3], rp.at[core, quarter[3]]))
     far_passed += [pass_far(slot) for slot in range(4, 8)]
     x_quarter(3)
     y_quarter(3)
-    far_passed += [pass_far(slot) for slot in range(8, 12)]
     y_sum = acc_y[:, 0:W] + acc_y[:, W : 2 * W]
-    ret_y[...] = jnp.transpose(jnp.concatenate([y_sum, y_sum], axis=1))[0:W]
-    ret_r[...] = acc_rt[:, 0:W, :] + acc_rt[:, W : 2 * W, :]
+    ret_y[...] = jnp.transpose(jnp.concatenate([y_sum, y_sum], axis=1))[0:W].astype(BF16)
+    ret_r[...] = (acc_rt[:, 0:W, :] + acc_rt[:, W : 2 * W, :]).astype(BF16)
     back_y = copies.start(ret_y, in_y, left)
     for j in range(2):
         copies.start(ret_r.at[j], in_r.at[core], at(1, j), COPIES - 2 + core)
 
-    arrive(far_tails)
-    arrive(far_passed)
-
-    @pl.loop(0, 12)
-    def _(slot):
-        mask = pick_lane(x_mask, 12 + slot)
-        f_tail = far[slot, :, D:MESSAGE].astype(F32)
-        f_w = jnp.where(low_lane, f_tail * mask, 0.0).astype(BF16)
-        f_t = jnp.transpose(f_tail)
-        f_a = f_t[W : W + 1] + f_t[W + 1 : W + 2] + f_t[W + 2 : W + 3]
-        f_p = far[slot, :, 0:D]
-        for t in range(4):
-            block(
-                got[quarter[t], 0:D], acol[quarter[t], :], None,
-                f_p, f_a, f_w, acc_x.at[quarter[t]], None,
-            )
-
+    far_passed += [pass_far(slot) for slot in range(8, 12)]
+    far_level(1)
+    far_level(2)
     back_m.wait_recv()
     back_y.wait_recv()
     for j in range(2):
         remote(
             ret_r.at[j], in_r.at[j], send_sem.at[COPIES - 1], recv_sem.at[COPIES - 2 + j], left
         ).wait_recv()
-    total = acc_xt[0:W, :] + in_m[...] + in_y[...] + in_r[0] + in_r[1]
+    total = acc_xt[0:W, :] + in_m[...] + in_y[...].astype(F32)
+    total = total + in_r[0].astype(F32) + in_r[1].astype(F32)
     total = jnp.transpose(jnp.concatenate([total, total], axis=0))
     x_sum = acc_x[...]
     total = total + x_sum + pltpu.roll(x_sum, W, 1)
@@ -495,7 +493,7 @@
 
     @pl.loop(1, LEAVES)
     def _(d):
-        other = lax.rem(me + d, LEAVES)
+        other = lax.rem(me + d * STRIDE, LEAVES)
         remote(back.at[other], home.at[me], all_sem.at[2], all_sem.at[3], other).start()
 
     home[me] = back[me]
@@ -548,8 +546,8 @@
             vmem(2, N, 128), vmem(2, N, 128), vmem(N, 128), vmem(N, 128),
             vmem(N, 128, dtype=F32), vmem(N, 128, dtype=F32),
             vmem(128, N, dtype=F32), vmem(128, N, dtype=F32), vmem(2, 128, N, dtype=F32),
-            vmem(W, N, dtype=F32), vmem(W, N, dtype=F32), vmem(2, W, N, dtype=F32),
-            vmem(W, N, dtype=F32), vmem(W, N, dtype=F32), vmem(2, W, N, dtype=F32),
+            vmem(W, N, dtype=F32), vmem(W, N), vmem(2, W, N),
+            vmem(W, N, dtype=F32), vmem(W, N), vmem(2, W, N),
             vmem(LEAVES, PEER, 128), vmem(LEAVES, PEER, 128),
             pltpu.SemaphoreType.DMA((COPIES,)), pltpu.SemaphoreType.DMA((COPIES,)),
             pltpu.SemaphoreType.DMA((4,)),

time: 181 us -> 170 us (0.939); the launches traced: 181 us -> 168 us
  Pallas kernels: 179 us -> 166 us
    pallas_call x1, Pallas kernels: 179 us -> 166 us  [local(): pl.pallas_call(tree_kernel, out_shape=jax.ShapeDtypeStruct((W, N), F32),...]
where the time goes in v3:
time: 170 us; the launch traced here: 168 us
  Pallas kernels  166 us (98%)
    pallas_call x1, Pallas kernels, local(): pl.pallas_call(tree_kernel, out_shape=jax.ShapeDtypeStruct((W, N), F32),...  166 us

profile of v3, /device:TPU:1, one launch (start us, length us, event | category | flops | bytes accessed | tf_op | source)
XLA Modules:
  0.0 167.7 jit_solution(9332543107802646687)
XLA Ops:
  0.0 165.5 %tree.1 = f32[64,1024]{1,0:T(8,128)} custom-call(s32[1,1024]{1,0:T(1,128)} %bitcast.9, bf16[64,1024]{1,0:T(8,128)(2,1)} %bitcast.8, bf16[1024,768]{1,0:T(8,128)(2,1)} %points.1, bf16[256,1024]{1,0:T(8,128)(2,1)} %bitcast.6, s32[1,256]{1,0:T(1,128)} %skel_row.1, bf16[240,512]{1,0:T(8,128)(2,1)} %bitcast.7, s32[1,240]{1,0:T(1,128)} %merge_i.1, ...), custom_call_target="tpu_custom_call" | custom-call | tf_op jit(solution)/shard_map/tree/pallas_call | solution.py:528
  165.5 1.7 copy.11
